TPU v7x, 128 devices: a whole 4x4x4 slice. The times are simulated.
128 devices in a mesh: prow: 8 (over y, core), pcol: 16 (over x, z).
Axes of the slice: x: 4, y: 4, z: 4, core: 2. Of those that a mesh axis runs over, the one named last changes fastest.
Arguments:
- assembly: float32 [8, 512, 2, 128, 128], P('prow', 'pcol'), may hold values from -6 to 6
- slot_tile: int32 [8, 512], P('prow', 'pcol'), may hold values from 0 to 511, as said below
- pivots: int32 [2, 128], replicated, may hold values from 0 to 16383, as said below
- inverses: float32 [2, 2, 128, 128], replicated, may hold values from -0.046875 to 0.046875
Outputs:
- factored: float32 [2, 16384, 4096], P(None, 'prow', 'pcol')
Inputs may be any that keep to these rules, and one draw needn't show every extreme that they name: `slot_tile`: row p lists tile ids t = i*32 + b, i the row tile among those of prow p and b the column tile; each of prow p's tiles appears in exactly one slot. A device's 32 slots hold at most 3 tiles whose column owner b % 16 is one index, and every device holds exactly 3 for some owner. `pivots`: entry j of panel k is either k*128 + j (no swap) or a row at or past 2*128; the rows named in one panel differ.
All inputs are finite; a program needn't handle non-finite values.
Results may differ from a plain program's by a relative error of at most 0.00013.
Values sent between devices are 32-bit elements; how exact they have to be, the bound alone decides.
A program may use at most 128 MiB of HBM per device.

v0:
```python
import jax
import jax.numpy as jnp
from jax import lax
from jax.sharding import PartitionSpec as P

CBLK = 2


def spread(x, axis, root):
    mine = lax.axis_index(axis) == root
    return lax.psum(jnp.where(mine, x, jnp.zeros_like(x)), axis)


def product(left, right):
    return jnp.dot(left, right, precision=lax.Precision.HIGHEST, preferred_element_type=jnp.float32)


def complex_product(left, right):
    real = product(left[0], right[0]) - product(left[1], right[1])
    imag = product(left[0], right[1]) + product(left[1], right[0])
    return jnp.stack([real, imag])


def per_device(assembly, slot_tile, pivots, inverses):
    cols_n = lax.axis_size("pcol")
    rows_n = lax.axis_size("prow")
    my_col = lax.axis_index("pcol")
    my_row = lax.axis_index("prow")
    tiles = assembly[0]
    slot_count = tiles.shape[0]
    block = tiles.shape[-1]
    width_tiles = CBLK * cols_n
    capacity = (slot_count + cols_n - 1) // cols_n + 1
    ident = slot_tile[0]
    column_tile = ident % width_tiles
    target = column_tile % cols_n
    local_id = ident // width_tiles * CBLK + column_tile // cols_n
    onehot = (target[:, None] == jnp.arange(cols_n, dtype=jnp.int32)[None, :]).astype(jnp.int32)
    before = jnp.cumsum(onehot, axis=0) - onehot
    rank = jnp.sum(before * onehot, axis=1)
    position = target * capacity + rank
    outgoing = (
        jnp.zeros((cols_n * capacity,) + tiles.shape[1:], jnp.float32).at[position].set(tiles)
    )
    labels = jnp.full((cols_n * capacity,), float(slot_count), jnp.float32)
    labels = labels.at[position].set(local_id.astype(jnp.float32))
    arrived, arrived_ids = (
        lax.all_to_all(outgoing, "pcol", split_axis=0, concat_axis=0, tiled=True),
        lax.all_to_all(labels, "pcol", split_axis=0, concat_axis=0, tiled=True),
    )
    placed = jnp.zeros_like(tiles).at[arrived_ids.astype(jnp.int32)].set(arrived, mode="drop")
    row_tiles = slot_count // CBLK
    row_total = row_tiles * block
    matrix = placed.reshape(row_tiles, CBLK, 2, block, block).transpose(2, 0, 3, 1, 4)
    matrix = matrix.reshape(2, row_total, CBLK * block)
    row_global = jnp.arange(row_total, dtype=jnp.int32) // block * rows_n + my_row
    col_global = jnp.arange(CBLK * block, dtype=jnp.int32) // block * cols_n + my_col
    for panel in range(2):
        chosen = pivots[panel]
        owner = chosen // block % rows_n
        where_local = chosen // block // rows_n * block + chosen % block
        mine = owner == my_row
        moved = chosen != panel * block + jnp.arange(block, dtype=jnp.int32)
        picked = jnp.where(
            mine[None, :, None], matrix[:, jnp.clip(where_local, 0, row_total - 1), :], 0.0
        )
        own_top = matrix[:, :block, :]
        old_top = spread(own_top, "prow", panel)
        new_top = lax.psum(picked, "prow")
        target_rows = jnp.where(mine & moved, where_local, row_total)
        matrix = matrix.at[:, target_rows, :].set(old_top, mode="drop")
        matrix = matrix.at[:, :block, :].set(
            jnp.where(my_row == panel, new_top, matrix[:, :block, :])
        )
        factor_block = inverses[panel]
        lower = row_global > panel
        right = col_global > panel
        panel_cols = matrix[:, :, :block]
        factor_rows = spread(complex_product(panel_cols, factor_block), "pcol", panel)
        update = complex_product(factor_rows, new_top)
        keep = lower[:, None] & right[None, :]
        matrix = matrix - jnp.where(keep[None], update, 0.0)
        stored = jnp.where(
            lower[None, :, None] & (my_col == panel), factor_rows, matrix[:, :, :block]
        )
        matrix = matrix.at[:, :, :block].set(stored)
    return matrix


def solution(mesh):
    in_specs = (P("prow", "pcol", None, None, None), P("prow", "pcol"), P(), P())
    out_specs = P(None, "prow", "pcol")
    return jax.shard_map(
        per_device, mesh=mesh, in_specs=in_specs, out_specs=out_specs, check_vma=False
    )
```

profile of v0, /device:TPU:20, one launch (start us, length us, event | category | flops | bytes accessed | tf_op | source)
XLA Modules:
  0.0 581.7 jit_solution(11028369693622349067)
XLA Ops:
  6.5 0.7 add_convert_fusion
  7.2 0.1 fusion.40
  7.3 0.1 reduce_window_sum.11
  7.3 0.2 select_reduce_fusion
  7.5 0.7 fusion.60
  8.2 0.7 scatter_custom_fusion
  8.9 0.7 all_to_all.9
  9.6 8.3 %all-to-all-start = ((f32[16,3,1]{1,2,0:T(1,128)}), f32[16,3,1]{1,2,0:T(1,128)S(1)}, u32[]{:S(2)}, u32[]{:S(2)}) async-start(f32[16,3,1]{1,2,0:T(1,128)} %bitcast.4), calls=%async_computation | async-start | bytes 16384 | tf_op jit(solution)/shard_map/all_to_all | solution.py:49
  17.9 3.4 broadcast_in_dim.82
  21.3 8.3 %scatter_fusion = f32[48,2,128,128]{3,2,1,0:T(8,128)} fusion(f32[48,2,128,128]{3,2,1,0:T(8,128)} %broadcast_in_dim.82, s32[32]{0:T(128)S(1)} %fusion.60, f32[32,2,128,128]{3,2,1,0:T(8,128)} %bitcast.194), kind=kCustom, calls=%fused_computation.3 | custom fusion | bytes 12583040 | tf_op jit(solution)/shard_map/scatter | solution.py:43
  29.6 7.4 %all-to-all-start.1 = ((f32[48,2,128,128]{3,2,1,0:T(8,128)}), f32[48,2,128,128]{3,2,1,0:T(8,128)}, u32[]{:S(2)}, u32[]{:S(2)}) async-start(f32[48,2,128,128]{3,2,1,0:T(8,128)} %scatter_fusion), calls=%async_computation.1 | async-start | bytes 12582912 | tf_op jit(solution)/shard_map/all_to_all | solution.py:48
  37.2 0.1 convert_element_type.22
  37.3 89.5 %all-to-all-done.1 = f32[48,2,128,128]{3,2,1,0:T(8,128)} async-done(((f32[48,2,128,128]{3,2,1,0:T(8,128)}), f32[48,2,128,128]{3,2,1,0:T(8,128)}, u32[]{:S(2)}, u32[]{:S(2)}) %all-to-all-start.1) | async-done | bytes 6291488 | tf_op jit(solution)/shard_map/all_to_all | solution.py:48
  126.9 2.5 broadcast_in_dim.80
  129.4 11.4 %scatter_fusion.1 = f32[32,2,128,128]{3,2,1,0:T(8,128)} fusion(f32[32,2,128,128]{3,2,1,0:T(8,128)} %broadcast_in_dim.80, s32[48]{0:T(128)S(1)} %fusion.61, f32[48,2,128,128]{3,2,1,0:T(8,128)} %all-to-all-done.1), kind=kCustom, calls=%fused_computation.4 | custom fusion | bytes 18874560 | tf_op jit(solution)/shard_map/scatter | solution.py:51
  140.8 7.5 %copy.27 = f32[2,16,128,2,128]{4,3,2,1,0:T(2,128)} copy(f32[2,16,128,2,128]{4,2,0,3,1:T(8,128)} %bitcast.193) | data formatting | bytes 8388608 | tf_op jit(solution)/shard_map/transpose | solution.py:54
  148.3 6.4 %reshape.911 = f32[2,2048,256]{2,1,0:T(8,128)} reshape(f32[2,16,128,2,128]{4,3,2,1,0:T(2,128)} %copy.27) | data formatting | bytes 8388608 | tf_op jit(solution)/shard_map/reshape | solution.py:55
  154.7 8.7 %copy.28 = f32[2,2048,256]{2,0,1:T(2,128)} copy(f32[2,2048,256]{2,1,0:T(8,128)} %reshape.911) | data formatting | bytes 8388608 | tf_op jit(solution)/shard_map/reshape | solution.py:55
  163.5 1.7 slice_select_fusion.5
  165.2 3.1 gather_fusion
  168.2 0.8 fusion.23
  169.1 0.3 all-reduce.7.cloned.1.call-start
  169.4 69.3 %all-reduce.13.cloned.1.call-done = (f32[2,128,256]{2,1,0:T(8,128)}, f32[2,128,256]{2,1,0:T(8,128)}) async-done(((f32[2,128,256]{2,1,0:T(8,128)}, f32[2,128,256]{2,1,0:T(8,128)}), (f32[2,128,256]{2,1,0:T(8,128)}, f32[2,128,256]{2,1,0:T(8,128)})) %all-reduce.13.cloned.1.call-update) | async-done | bytes 524304 | tf_op jit(solution)/shard_map/psum | solution.py:11
  238.6 1.2 copy.29
  239.8 12.7 %scatter_fusion.2 = f32[2,2048,256]{2,0,1:T(2,128)} fusion(f32[2,2048,256]{2,0,1:T(2,128)} %copy.28, s32[128]{0:T(128)S(1)} %fusion.62, f32[128,2,256]{2,1,0:T(2,128)S(1)} %copy.29), kind=kCustom, calls=%fused_computation.5 | custom fusion | bytes 786944 | tf_op jit(solution)/shard_map/scatter | solution.py:71
  252.5 2.6 copy.33
  255.1 0.1 fusion.21
  255.2 1.0 fusion.13
  256.2 1.0 fusion.12
  257.1 1.0 fusion.9
  258.1 1.0 fusion.8
  259.1 1.4 maximum_select_fusion.2
  260.6 0.0 all-reduce.11.cloned.1.call-start
  260.7 0.5 broadcast_and_fusion.1
  261.2 94.4 %all-reduce.7.cloned.1.call-done = f32[2,2048,128]{2,1,0:T(8,128)} async-done(((f32[2,2048,128]{2,1,0:T(8,128)}), f32[2,2048,128]{2,1,0:T(8,128)}) %all-reduce.7.cloned.1.call-update) | async-done | bytes 2097168 | tf_op jit(solution)/shard_map/psum | solution.py:11
  355.6 3.2 fusion.15
  358.8 3.0 fusion.14
  361.9 1.8 fusion.5
  363.8 1.8 fusion.4
  365.6 0.6 fusion
  366.2 0.7 fusion.11
  366.9 12.2 %copy.34 = f32[2,2048,256]{2,0,1:T(2,128)} copy(f32[2,2048,256]{2,1,0:T(8,128)S(1)} %fusion.11) | data formatting | bytes 8388608 | tf_op jit(solution)/shard_map/scatter | solution.py:86
  379.1 0.7 slice_select_fusion.3
  379.8 3.1 gather_fusion.1
  382.9 0.8 fusion.22
  383.7 9.9 %all-reduce.9.cloned.1.call-start = ((), (), s32[]{:S(2)}) async-start(), calls=%async_computation.3 | async-start | bytes 4194304 | tf_op jit(solution)/shard_map/psum | solution.py:11
  393.6 48.4 %all-reduce.11.cloned.1.call-done = (f32[2,128,256]{2,1,0:T(8,128)}, f32[2,128,256]{2,1,0:T(8,128)}) async-done(((f32[2,128,256]{2,1,0:T(8,128)}, f32[2,128,256]{2,1,0:T(8,128)}), (f32[2,128,256]{2,1,0:T(8,128)}, f32[2,128,256]{2,1,0:T(8,128)})) %all-reduce.11.cloned.1.call-update) | async-done | bytes 524304 | tf_op jit(solution)/shard_map/psum | solution.py:11
  442.0 1.2 copy.35
  443.1 15.2 %scatter_fusion.3 = f32[2,2048,256]{2,0,1:T(2,128)} fusion(f32[2,2048,256]{2,0,1:T(2,128)} %copy.34, s32[128]{0:T(128)S(1)} %get-tuple-element.67, f32[128,2,256]{2,1,0:T(2,128)S(1)} %copy.35), kind=kCustom, calls=%fused_computation.6 | custom fusion | bytes 786944 | tf_op jit(solution)/shard_map/scatter | solution.py:71
  458.3 2.6 copy.39
  460.9 0.1 fusion.20
  461.0 1.0 fusion.17
  461.9 1.0 fusion.16
  462.9 1.0 fusion.7
  463.9 1.0 fusion.6
  464.9 1.4 maximum_select_fusion.3
  466.4 0.5 broadcast_and_fusion
  466.9 92.7 %all-reduce.9.cloned.1.call-done = f32[2,2048,128]{2,1,0:T(8,128)} async-done(((f32[2,2048,128]{2,1,0:T(8,128)}), f32[2,2048,128]{2,1,0:T(8,128)}) %all-reduce.9.cloned.1.call-update) | async-done | bytes 2097168 | tf_op jit(solution)/shard_map/psum | solution.py:11
  559.6 3.2 fusion.19
  562.8 3.0 fusion.18
  565.9 1.8 fusion.3
  567.7 1.8 fusion.2
  569.6 2.7 fusion.1
  572.2 2.8 fusion.10
  (41 shorter events, 0.3 us)
Async XLA Ops:
  9.6 20.1 %all-to-all-start = ((f32[16,3,1]{1,2,0:T(1,128)}), f32[16,3,1]{1,2,0:T(1,128)S(1)}, u32[]{:S(2)}, u32[]{:S(2)}) async-start(f32[16,3,1]{1,2,0:T(1,128)} %bitcast.4), calls=%async_computation | async-start | bytes 16384 | tf_op jit(solution)/shard_map/all_to_all | solution.py:49
  29.6 7.5 %copy-start.9 = (s32[2,128]{1,0:T(2,128)S(1)}, s32[2,128]{1,0:T(2,128)}, u32[]{:S(2)}) copy-start(s32[2,128]{1,0:T(2,128)} %param.14) | copy-start | bytes 3076
  29.6 97.3 %all-to-all-start.1 = ((f32[48,2,128,128]{3,2,1,0:T(8,128)}), f32[48,2,128,128]{3,2,1,0:T(8,128)}, u32[]{:S(2)}, u32[]{:S(2)}) async-start(f32[48,2,128,128]{3,2,1,0:T(8,128)} %scatter_fusion), calls=%async_computation.1 | async-start | bytes 12582912 | tf_op jit(solution)/shard_map/all_to_all | solution.py:48
  37.0 201.6 %all-reduce.13.cloned.1.call-start = ((), (), s32[]{:S(2)}) async-start(), calls=%async_computation.5 | async-start | bytes 1048576 | tf_op jit(solution)/shard_map/psum | solution.py:11
  169.1 186.6 %all-reduce.7.cloned.1.call-start = ((), (), s32[]{:S(2)}) async-start(), calls=%async_computation.2 | async-start | bytes 4194304 | tf_op jit(solution)/shard_map/psum | solution.py:11
  252.5 2.6 copy-start.6
  252.5 2.7 copy-start.8
  255.2 4.0 copy-start
  260.6 181.3 %all-reduce.11.cloned.1.call-start = ((), (), s32[]{:S(2)}) async-start(), calls=%async_computation.4 | async-start | bytes 1048576 | tf_op jit(solution)/shard_map/psum | solution.py:11
  355.6 6.3 %copy-start.4 = (f32[2,2048,128]{2,1,0:T(8,128)S(1)}, f32[2,2048,128]{2,1,0:T(8,128)}, u32[]{:S(2)}) copy-start(f32[2,2048,128]{2,1,0:T(8,128)} %all-reduce.7.cloned.1.call-done) | copy-start | bytes 6291460
  361.9 3.7 copy-start.1
  383.7 175.9 %all-reduce.9.cloned.1.call-start = ((), (), s32[]{:S(2)}) async-start(), calls=%async_computation.3 | async-start | bytes 4194304 | tf_op jit(solution)/shard_map/psum | solution.py:11
  458.3 2.6 copy-start.7
  460.9 4.0 copy-start.2
  559.6 6.3 %copy-start.5 = (f32[2,2048,128]{2,1,0:T(8,128)S(1)}, f32[2,2048,128]{2,1,0:T(8,128)}, u32[]{:S(2)}) copy-start(f32[2,2048,128]{2,1,0:T(8,128)} %all-reduce.9.cloned.1.call-done) | copy-start | bytes 6291460
  565.9 3.7 copy-start.3
Sparse Core Ops, SparseCore 0:
  169.2 69.4 all-reduce.12
  260.7 94.8 all-reduce.6
  383.8 58.0 all-reduce.10
  466.5 93.0 all-reduce.8
where the time goes:
time: 592 us; the launch traced here: 582 us
  waiting for transfers between devices  394 us (67%)
  local copies, waits for them, and re-layouts  104 us (18%)
  matrix products  27.6 us (5%)
  starting transfers between devices  25.9 us (4%)
  other arithmetic  16.5 us (3%)
  between operations  13.8 us (2%)
    psum x4, waiting for transfers between devices, spread(): return lax.psum(jnp.where(mine, x, jnp.zeros_like(x)), axis)  305 us
    all_to_all x1, waiting for transfers between devices, per_device(): lax.all_to_all(outgoing, 'pcol', split_axis=0, concat_axis=0, tiled=True)  89.5 us
    scatter x4, local copies, waits for them, and re-layouts, per_device(): matrix = matrix.at[:, target_rows, :].set(old_top, mode='drop')  33 us
    dot_general x16, matrix products, product(): jnp.dot(left, right, precision=lax.Precision.HIGHEST, preferred_element_t...  27.6 us
    reshape x2, local copies, waits for them, and re-layouts, per_device(): matrix = matrix.reshape(2, row_total, CBLK * block)  15.2 us
    scatter x1, local copies, waits for them, and re-layouts, per_device(): matrix = matrix.at[:, :, :block].set(stored)  12.2 us
  transfers between devices with their start and end apart: 6, of which 5 were waited for; matrix products, arithmetic and copies ran while one was open for 2% of the time, Pallas kernels for 0%

commit v1 on v0

v1 whole, which is shorter than its diff:
```python
import functools

import jax
import jax.numpy as jnp
from jax import lax
from jax.experimental import pallas as pl
from jax.experimental.pallas import tpu as pltpu
from jax.sharding import PartitionSpec as P

CBLK = 2
NB = 128
MESH = pl.DeviceIdType.MESH
HI = lax.Precision.HIGHEST


def comm_kernel(
    dims, idx_ref, piv_ref, lab_ref, asm_hbm,
    m_hbm, ag_hbm, fin_hbm, wfin_hbm,
    asm, sendb, recvb, labs, mat, pb, ag, pk, rb, fin, wfin, place,
    out_sem, lab_s, lab_r, a_s, a_r, sc_s, sc_r, rs_s, rs_r, t_s, t_r, y_s, y_r, wb_s, wb_r, wy_s, wy_r,
    g1_s, g1_r, g2_s, g2_r,
):
    rows_n, nx, nz, cap, row_tiles = dims
    cols_n = nx * nz
    sl = NB // rows_n
    half = NB // 2
    me_r = lax.axis_index("prow")
    me_c = lax.axis_index("pcol")
    me_x = me_c // nz
    me_z = me_c % nz

    def remote(src, dst, ssem, rsem, row, col):
        return pltpu.make_async_remote_copy(
            src_ref=src, dst_ref=dst, send_sem=ssem, recv_sem=rsem,
            device_id=(row, col), device_id_type=MESH)

    load = pltpu.make_async_copy(asm_hbm, asm, out_sem.at[4])
    load.start()

    barrier = pltpu.get_barrier_semaphore()

    def greet_col(k, c):
        pl.semaphore_signal(barrier, inc=1, device_id=(me_r, (me_c + k) % cols_n), device_id_type=MESH)
        return c

    def greet_row(k, c):
        pl.semaphore_signal(barrier, inc=1, device_id=((me_r + k) % rows_n, me_c), device_id_type=MESH)
        return c

    lax.fori_loop(1, cols_n, greet_col, 0)
    lax.fori_loop(1, rows_n, greet_row, 0)
    pl.semaphore_wait(barrier, cols_n - 1 + rows_n - 1)

    def lab_copy(d):
        return remote(lab_ref, labs.at[me_c], lab_s.at[d], lab_r.at[me_c], me_r, d)

    def lab_start(k, c):
        lab_copy((me_c + k) % cols_n).start()
        return c

    lax.fori_loop(1, cols_n, lab_start, 0)
    labs[me_c] = lab_ref[...]
    load.wait()

    def a_copy(d):
        return remote(sendb.at[d], recvb.at[me_c], a_s.at[d], a_r.at[me_c], me_r, d)

    for r in range(cap):
        recvb[me_c, r] = asm[idx_ref[me_c * cap + r]]

    def pack(k, c):
        d = (me_c + k) % cols_n
        for r in range(cap):
            sendb[d, r] = asm[idx_ref[d * cap + r]]

        @pl.when(k > 1)
        def _():
            a_copy((me_c + k - 1) % cols_n).start()
        return c

    lax.fori_loop(1, cols_n, pack, 0)
    a_copy((me_c + cols_n - 1) % cols_n).start()

    def lab_wait(k, c):
        s = (me_c + k) % cols_n
        remote(lab_ref, labs.at[s], lab_s.at[s], lab_r.at[s], me_r, s).wait_recv()
        return c

    lax.fori_loop(1, cols_n, lab_wait, 0)
    seen = labs[:, 0, :]
    lane = lax.broadcasted_iota(jnp.int32, seen.shape, 1) - me_c * cap
    code = lax.broadcasted_iota(jnp.int32, seen.shape, 0) * cap + lane
    code = jnp.where((lane >= 0) & (lane < cap), code, 0)
    valid = jnp.where((lane >= 0) & (lane < cap), seen, -1)

    def find(t, c):
        place[t] = jnp.minimum(jnp.sum(jnp.where(valid == t, code, 0)), cols_n * cap - 1)
        return c

    lax.fori_loop(0, row_tiles * CBLK, find, 0)

    def a_wait(k, c):
        s = (me_c + k) % cols_n
        remote(sendb.at[s], recvb.at[s], a_s.at[s], a_r.at[s], me_r, s).wait_recv()
        return c

    lax.fori_loop(1, cols_n, a_wait, 0)

    def put(i, c):
        rows = pl.ds(pl.multiple_of(i * NB, NB), NB)
        for m in range(CBLK):
            at = place[i * CBLK + m]
            s = at // cap
            r = at - s * cap
            re = recvb[s, r, 0]
            im = recvb[s, r, 1]
            mat[rows, m * NB:(m + 1) * NB] = re
            mat[rows, (CBLK + m) * NB:(CBLK + m + 1) * NB] = im
            if m == 0:
                pb[i, :, 0:NB] = re
                pb[i, :, NB:2 * NB] = im
        return c

    lax.fori_loop(0, row_tiles, put, 0)
    m_out = pltpu.make_async_copy(mat, m_hbm, out_sem.at[0])
    m_out.start()

    def sc_copy(b, d):
        return remote(pb.at[d], ag.at[b, d // nz, d % nz], sc_s.at[d], sc_r.at[b], me_r, d)

    for b in range(2):
        @pl.when(me_c == b)
        def _():
            def go(k, c):
                sc_copy(b, (b + k) % cols_n).start()
                return c
            lax.fori_loop(1, cols_n, go, 0)
            ag[b, b // nz, b % nz] = pb[b]

    def pick(d, c):
        def one(jj, c2):
            for k in range(2):
                r = piv_ref[k, d * sl + jj]
                tile = r // NB
                mine = (tile % rows_n) == me_r
                loc = tile // rows_n * NB + r % NB
                row = mat[pl.ds(loc, 1), :]
                pk[d, pl.ds(k * sl + jj, 1), :] = jnp.where(mine, row, 0.0)
            return c2
        return lax.fori_loop(0, sl, one, c)

    lax.fori_loop(0, rows_n, pick, 0)

    def rs_copy(d):
        return remote(pk.at[d], rb.at[me_r], rs_s.at[d], rs_r.at[me_r], d, me_c)

    def rs_start(k, c):
        rs_copy((me_r + k) % rows_n).start()
        return c

    lax.fori_loop(1, rows_n, rs_start, 0)

    def t_copy(s, d):
        rows = pl.ds(pl.multiple_of(d * sl, sl), sl)
        return remote(mat.at[rows, :], fin.at[d, pl.ds((2 + s) * sl, sl), :], t_s.at[d], t_r.at[s], d, me_c)

    for s in range(2):
        @pl.when(me_r == s)
        def _():
            def go(k, c):
                t_copy(s, (s + k) % rows_n).start()
                return c
            lax.fori_loop(1, rows_n, go, 0)
            fin[s, (2 + s) * sl:(3 + s) * sl, :] = mat[s * sl:(s + 1) * sl, :]

    def rs_wait(k, c):
        s = (me_r + k) % rows_n
        remote(pk.at[s], rb.at[s], rs_s.at[s], rs_r.at[s], s, me_c).wait_recv()
        return c

    lax.fori_loop(1, rows_n, rs_wait, 0)
    total = pk[me_r]

    def add(k, acc):
        return acc + rb[(me_r + k) % rows_n]

    fin[me_r, 0:2 * sl, :] = lax.fori_loop(1, rows_n, add, total)
    for s in range(2):
        @pl.when(me_r != s)
        def _():
            part = fin.at[me_r, pl.ds((2 + s) * sl, sl), :]
            remote(part, part, t_s.at[s], t_r.at[s], s, me_c).wait_recv()

    def y_copy(d):
        return remote(fin.at[me_r], fin.at[me_r], y_s.at[d], y_r.at[me_r], d, me_c)

    def y_start(k, c):
        y_copy((me_r + k) % rows_n).start()
        return c

    lax.fori_loop(1, rows_n, y_start, 0)

    def wb_copy(b, d):
        return remote(wfin.at[b, me_r], wfin.at[b, me_r], wb_s.at[d], wb_r.at[b], me_r, d)

    for b in range(2):
        @pl.when(me_c == b)
        def _():
            wfin[b, me_r, :, 0:NB] = fin[me_r, :, 0:NB]
            wfin[b, me_r, :, NB:2 * NB] = fin[me_r, :, CBLK * NB:(CBLK + 1) * NB]

            def go(k, c):
                wb_copy(b, (b + k) % cols_n).start()
                return c
            lax.fori_loop(1, cols_n, go, 0)

    for b in range(2):
        @pl.when(me_c != b)
        def _():
            part = ag.at[b, me_x, me_z]
            remote(part, part, sc_s.at[b], sc_r.at[b], me_r, b).wait_recv()

    lo = pl.ds(0, half)
    hi = pl.ds(half, half)

    def g1x(dx):
        part = ag.at[:, me_x, me_z, lo, :]
        return remote(part, part, g1_s.at[0, dx], g1_r.at[0, me_x], me_r, dx * nz + me_z)

    def g1z(dz):
        part = ag.at[:, me_x, me_z, hi, :]
        return remote(part, part, g1_s.at[1, dz], g1_r.at[1, me_z], me_r, me_x * nz + dz)

    def g2z(dz):
        part = ag.at[:, :, me_z, lo, :]
        return remote(part, part, g2_s.at[0, dz], g2_r.at[0, me_z], me_r, me_x * nz + dz)

    def g2x(dx):
        part = ag.at[:, me_x, :, hi, :]
        return remote(part, part, g2_s.at[1, dx], g2_r.at[1, me_x], me_r, dx * nz + me_z)

    for k in range(1, nx):
        g1x((me_x + k) % nx).start()
    for k in range(1, nz):
        g1z((me_z + k) % nz).start()

    for b in range(2):
        @pl.when(me_c != b)
        def _():
            part = wfin.at[b, me_r]
            remote(part, part, wb_s.at[b], wb_r.at[b], me_r, b).wait_recv()

    def wy_copy(d):
        part = wfin.at[:, me_r]
        return remote(part, part, wy_s.at[d], wy_r.at[me_r], d, me_c)

    def wy_start(k, c):
        wy_copy((me_r + k) % rows_n).start()
        return c

    lax.fori_loop(1, rows_n, wy_start, 0)

    for k in range(1, nx):
        sx = (me_x + k) % nx
        part = ag.at[:, sx, me_z, lo, :]
        remote(part, part, g1_s.at[0, sx], g1_r.at[0, sx], me_r, sx * nz + me_z).wait_recv()
    for k in range(1, nz):
        g2z((me_z + k) % nz).start()
    for k in range(1, nz):
        sz = (me_z + k) % nz
        part = ag.at[:, me_x, sz, hi, :]
        remote(part, part, g1_s.at[1, sz], g1_r.at[1, sz], me_r, me_x * nz + sz).wait_recv()
    for k in range(1, nx):
        g2x((me_x + k) % nx).start()

    def y_wait(k, c):
        s = (me_r + k) % rows_n
        part = fin.at[s]
        remote(part, part, y_s.at[s], y_r.at[s], s, me_c).wait_recv()
        part = wfin.at[:, s]
        remote(part, part, wy_s.at[s], wy_r.at[s], s, me_c).wait_recv()
        return c

    lax.fori_loop(1, rows_n, y_wait, 0)
    f_out = pltpu.make_async_copy(fin, fin_hbm, out_sem.at[1])
    f_out.start()
    w_out = pltpu.make_async_copy(wfin, wfin_hbm, out_sem.at[2])
    w_out.start()

    for k in range(1, nz):
        sz = (me_z + k) % nz
        part = ag.at[:, :, sz, lo, :]
        remote(part, part, g2_s.at[0, sz], g2_r.at[0, sz], me_r, me_x * nz + sz).wait_recv()
    for k in range(1, nx):
        sx = (me_x + k) % nx
        part = ag.at[:, sx, :, hi, :]
        remote(part, part, g2_s.at[1, sx], g2_r.at[1, sx], me_r, sx * nz + me_z).wait_recv()
    g_out = pltpu.make_async_copy(ag, ag_hbm, out_sem.at[3])
    g_out.start()

    def sent_col(k, c):
        d = (me_c + k) % cols_n
        lab_copy(d).wait_send()
        a_copy(d).wait_send()
        return c

    lax.fori_loop(1, cols_n, sent_col, 0)

    def sent_row(k, c):
        d = (me_r + k) % rows_n
        rs_copy(d).wait_send()
        y_copy(d).wait_send()
        wy_copy(d).wait_send()
        return c

    lax.fori_loop(1, rows_n, sent_row, 0)
    for b in range(2):
        @pl.when(me_c == b)
        def _():
            def go(k, c):
                d = (b + k) % cols_n
                sc_copy(b, d).wait_send()
                wb_copy(b, d).wait_send()
                return c
            lax.fori_loop(1, cols_n, go, 0)

        @pl.when(me_r == b)
        def _():
            def go(k, c):
                t_copy(b, (b + k) % rows_n).wait_send()
                return c
            lax.fori_loop(1, rows_n, go, 0)
    for k in range(1, nx):
        g1x((me_x + k) % nx).wait_send()
        g2x((me_x + k) % nx).wait_send()
    for k in range(1, nz):
        g1z((me_z + k) % nz).wait_send()
        g2z((me_z + k) % nz).wait_send()
    m_out.wait()
    f_out.wait()
    w_out.wait()
    g_out.wait()


def cmat(re, im):
    return jnp.concatenate([jnp.concatenate([re, im], 1), jnp.concatenate([-im, re], 1)], 0)


def dot(a, b):
    return jnp.dot(a, b, precision=HI, preferred_element_type=jnp.float32)


def per_device(dims, assembly, slot_tile, pivots, inverses):
    rows_n, nx, nz, cap, row_tiles = dims
    cols_n = nx * nz
    tiles = assembly[0]
    slots = tiles.shape[0]
    width_tiles = CBLK * cols_n
    ident = slot_tile[0]
    column_tile = ident % width_tiles
    target = column_tile % cols_n
    local_id = ident // width_tiles * CBLK + column_tile // cols_n
    num = jnp.arange(slots, dtype=jnp.int32)
    rank = jnp.sum(((target[:, None] == target[None, :]) & (num[None, :] < num[:, None])).astype(jnp.int32), axis=1)
    position = target * cap + rank
    hit = position[None, :] == jnp.arange(128, dtype=jnp.int32)[:, None]
    send_idx = jnp.sum(jnp.where(hit, num[None, :], 0), axis=1)
    labels = jnp.sum(jnp.where(hit, local_id[None, :] + 1, 0), axis=1) - 1
    labels = jnp.broadcast_to(labels[None, :], (8, 128))

    sl = NB // rows_n
    rows = row_tiles * NB
    wide = 2 * CBLK * NB
    f32 = jnp.float32
    dma = pltpu.SemaphoreType.DMA
    hbm = pl.BlockSpec(memory_space=pl.ANY)
    smem = pl.BlockSpec(memory_space=pltpu.SMEM)
    n = max(nx, nz)
    m_raw, ag, fin, wfin = pl.pallas_call(
        functools.partial(comm_kernel, dims),
        out_shape=(
            jax.ShapeDtypeStruct((rows, wide), f32),
            jax.ShapeDtypeStruct((2, nx, nz, NB, 2 * NB), f32),
            jax.ShapeDtypeStruct((rows_n, 4 * sl, wide), f32),
            jax.ShapeDtypeStruct((2, rows_n, 4 * sl, 2 * NB), f32),
        ),
        in_specs=[smem, smem, pl.BlockSpec(memory_space=pltpu.VMEM), hbm],
        out_specs=(hbm, hbm, hbm, hbm),
        scratch_shapes=[
            pltpu.VMEM((slots, 2, NB, NB), f32),
            pltpu.VMEM((cols_n, cap, 2, NB, NB), f32),
            pltpu.VMEM((cols_n, cap, 2, NB, NB), f32),
            pltpu.VMEM((cols_n, 8, 128), jnp.int32),
            pltpu.VMEM((rows, wide), f32),
            pltpu.VMEM((row_tiles, NB, 2 * NB), f32),
            pltpu.VMEM((2, nx, nz, NB, 2 * NB), f32),
            pltpu.VMEM((rows_n, 2 * sl, wide), f32),
            pltpu.VMEM((rows_n, 2 * sl, wide), f32),
            pltpu.VMEM((rows_n, 4 * sl, wide), f32),
            pltpu.VMEM((2, rows_n, 4 * sl, 2 * NB), f32),
            pltpu.SMEM((slots,), jnp.int32),
            dma((5,)),
            dma((cols_n,)), dma((cols_n,)),
            dma((cols_n,)), dma((cols_n,)),
            dma((cols_n,)), dma((2,)),
            dma((rows_n,)), dma((rows_n,)),
            dma((rows_n,)), dma((2,)),
            dma((rows_n,)), dma((rows_n,)),
            dma((cols_n,)), dma((2,)),
            dma((rows_n,)), dma((rows_n,)),
            dma((2, n)), dma((2, n)),
            dma((2, n)), dma((2, n)),
        ],
        compiler_params=pltpu.CompilerParams(
            collective_id=0, has_side_effects=True, vmem_limit_bytes=60 * 1024 * 1024),
        name="exchange",
    )(send_idx, pivots, labels, tiles)

    my_col = lax.axis_index("pcol")
    my_row = lax.axis_index("prow")
    sets = fin.reshape(rows_n, 4, sl, wide).transpose(1, 0, 2, 3).reshape(4, NB, wide)
    wsets = wfin.reshape(2, rows_n, 4, sl, 2 * NB).transpose(0, 2, 1, 3, 4).reshape(2, 4, NB, 2 * NB)
    wall = jnp.concatenate([sets, wsets[0], wsets[1]], -1)
    p0, p1, t0, t1 = wall[0], wall[1], wall[2], wall[3]
    i0 = cmat(inverses[0, 0], inverses[0, 1])
    i1 = cmat(inverses[1, 0], inverses[1, 1])

    def unpack(v):
        h = v.shape[1] // 2
        return cmat(v[:, :h], v[:, h:])

    both = (pivots[1][:, None] == pivots[0][None, :])
    e = both.astype(f32)
    p1 = jnp.where(jnp.any(both, 1)[:, None], dot(e, t0), p1)
    u0 = p0[:, :wide]
    u0b1 = p0[:, wide + 2 * NB:]
    l0p1 = dot(p1[:, wide:wide + 2 * NB], i0)
    u1 = p1[:, :wide] - dot(l0p1, unpack(u0))
    g = dot(dot(i0, unpack(u0b1)), i1)
    ru0, ru1 = unpack(u0), unpack(u1)
    h_lo = dot(i1, ru1)
    h_hi = dot(i0, ru0) - dot(g, ru1)
    col = jnp.arange(wide) % (CBLK * NB) // NB * cols_n + my_col
    is0 = col == 0
    is1 = col == 1

    def spreadc(v):
        pad = jnp.zeros((v.shape[0], NB), f32)
        return jnp.concatenate([v[:, :NB], pad, v[:, NB:], pad], 1)
    h_hi = jnp.where(is0[None, :], -spreadc(i0), jnp.where(is1[None, :], spreadc(g), h_hi))
    h_lo = jnp.where(is0[None, :], 0.0, jnp.where(is1[None, :], -spreadc(i1), h_lo))
    h = jnp.concatenate([h_hi, h_lo], 0)

    row_global = (jnp.arange(rows) // NB * rows_n + my_row) * NB + jnp.arange(rows) % NB
    hit0 = (row_global[:, None] == pivots[0][None, :]) & (row_global >= 2 * NB)[:, None]
    hit1 = (row_global[:, None] == pivots[1][None, :]) & (row_global >= 2 * NB)[:, None]
    in1 = jnp.any(hit1, 1)
    in0 = jnp.any(hit0, 1)
    hit0 = hit0 & ~in1[:, None]
    swap = dot(jnp.concatenate([hit0, hit1], 1).astype(f32), jnp.concatenate([t0, t1], 0))
    raw = jnp.concatenate([m_raw, ag[0].reshape(rows, 2 * NB), ag[1].reshape(rows, 2 * NB)], 1)
    z = jnp.where((in0 | in1)[:, None], swap, raw)
    out = jnp.where((is0 | is1)[None, :], 0.0, z[:, :wide]) - dot(z[:, wide:], h)
    row1 = jnp.where(is0[None, :], spreadc(l0p1), u1)
    top = jnp.where(my_row == 0, u0, jnp.where(my_row == 1, row1, out[:NB]))
    out = jnp.concatenate([top, out[NB:]], 0)
    return jnp.stack([out[:, :CBLK * NB], out[:, CBLK * NB:]])


def grid_of(cols_n):
    nx = 1
    while nx * nx < cols_n:
        nx *= 2
    return nx, cols_n // nx


def solution(mesh):
    rows_n, cols_n = mesh.shape["prow"], mesh.shape["pcol"]
    nx, nz = grid_of(cols_n)

    def body(assembly, slot_tile, pivots, inverses):
        slots = assembly.shape[1]
        cap = (slots + cols_n - 1) // cols_n + 1
        dims = (rows_n, nx, nz, cap, slots // CBLK)
        return per_device(dims, assembly, slot_tile, pivots, inverses)

    in_specs = (P("prow", "pcol", None, None, None), P("prow", "pcol"), P(), P())
    out_specs = P(None, "prow", "pcol")
    return jax.shard_map(body, mesh=mesh, in_specs=in_specs, out_specs=out_specs, check_vma=False)
```

time: 592 us -> 258 us (0.44); the launches traced: 582 us -> 256 us
  waiting for transfers between devices: 394 us -> 0 us
  Pallas kernels: 0 us -> 199 us
  local copies, waits for them, and re-layouts: 104 us -> 16.7 us
  starting transfers between devices: 25.9 us -> 0 us
  between operations: 13.8 us -> 0.34 us
    psum x4 -> x0, waiting for transfers between devices: 305 us -> none  [spread(): return lax.psum(jnp.where(mine, x, jnp.zeros_like(x)), axis)]
    pallas_call x0 -> x1, Pallas kernels: none -> 199 us  [per_device(): pl.pallas_call(functools.partial(comm_kernel, dims), out_shape=(jax.Shape...]
    all_to_all x2 -> x0, waiting for transfers between devices: 89.5 us -> none  [the longest x1 89.5 us: per_device(): lax.all_to_all(outgoing, 'pcol', split_axis=0, concat_axis=0, tiled=True)]
    scatter x8 -> x0, local copies, waits for them, and re-layouts: 65.6 us -> none  [the longest x4 33 us: per_device(): matrix = matrix.at[:, target_rows, :].set(old_top, mode='drop')]
    all_to_all x2 -> x0, starting transfers between devices: 15.7 us -> none  [the longest x1 8.3 us: per_device(): lax.all_to_all(labels, 'pcol', split_axis=0, concat_axis=0, tiled=True)]
    reshape x2 -> x0, local copies, waits for them, and re-layouts: 15.2 us -> none  [per_device(): matrix = matrix.reshape(2, row_total, CBLK * block)]
    psum x4 -> x0, starting transfers between devices: 10.2 us -> none  [spread(): return lax.psum(jnp.where(mine, x, jnp.zeros_like(x)), axis)]
    slice x0 -> x10, local copies, waits for them, and re-layouts: none -> 7.91 us  [the longest x1 2.66 us: per_device(): ag[0].reshape(rows, 2 * NB)]
  transfers between devices with their start and end apart: 6 -> 0, of which waited for: 5 -> 0; matrix products, arithmetic and copies ran while one was open for 2% -> 0% of each run, Pallas kernels for 0% -> 0%
where the time goes in v1:
time: 258 us; the launch traced here: 256 us
  Pallas kernels  199 us (77%)
  matrix products  24.1 us (9%)
  local copies, waits for them, and re-layouts  16.7 us (6%)
  other arithmetic  16.2 us (6%)
    pallas_call x1, Pallas kernels, per_device(): pl.pallas_call(functools.partial(comm_kernel, dims), out_shape=(jax.Shape...  199 us
    dot_general x10, matrix products, dot(): return jnp.dot(a, b, precision=HI, preferred_element_type=jnp.float32)  24.1 us
    unnamed x26, local copies, waits for them, and re-layouts  7.15 us

profile of v1, /device:TPU:20, one launch (start us, length us, event | category | flops | bytes accessed | tf_op | source)
XLA Modules:
  0.0 255.9 jit_solution(6527326065573467190)
XLA Ops:
  0.0 0.7 fusion.71
  0.7 0.7 and_select_fusion.2
  1.3 0.2 convert_reduce_fusion
  1.5 0.7 fusion.62
  2.2 0.6 select_reduce_fusion
  2.8 0.6 broadcast_in_dim.116.lab_ref
  3.4 198.5 %exchange.1 = (f32[2048,512]{1,0:T(8,128)}, f32[2,4,4,128,256]{4,3,2,1,0:T(8,128)}, f32[8,64,512]{2,1,0:T(8,128)}, f32[2,8,64,256]{3,2,1,0:T(8,128)}) custom-call(s32[128]{0:T(128)} %get-tuple-element.16.idx_ref, s32[2,128]{1,0:T(2,128)} %piv_ref.1, s32[8,128]{1,0:T(8,128)} %broadcast_in_dim.116.lab_ref, f32[32,2,128,128]{3,2,1,0:T(8,128)} %bitcast.54), custom_call_target="tpu_custom_call" | custom-call | tf_op jit(solution)/shard_map/exchange/pallas_call | solution.py:379
  202.0 0.0 copy-start.3
  202.0 1.4 fusion.76
  203.4 0.1 copy-done.3
  203.5 0.1 copy.12
  203.6 0.0 copy-start.9
  203.6 0.2 pad_maximum_fusion.2
  203.8 1.0 slice_bitcast_fusion.3
  204.8 0.0 copy-start.10
  204.8 0.7 fusion.77
  205.5 0.7 slice_negate_fusion.2
  206.2 0.0 copy-done.9
  206.2 0.7 fusion.80
  206.9 0.1 copy.20
  207.0 0.0 copy-start.5
  207.0 1.6 copy.19
  208.6 2.4 fusion.29
  211.0 0.0 copy-done.5
  211.0 0.9 copy.22
  211.9 0.6 bitcast_negate_fusion
  212.5 1.6 copy.21
  214.1 0.0 copy-start.6
  214.1 0.0 copy-start.7
  214.1 1.4 fusion.73
  215.5 0.0 copy-start.4
  215.5 1.0 maximum_maximum_fusion.6
  216.6 0.8 fusion.78
  217.4 2.7 %fusion.27 = f32[256,512]{0,1:T(8,128)} fusion(f32[128,256]{1,0:T(8,128)S(1)} %get-tuple-element.29, f32[128,256]{1,0:T(8,128)S(1)} %get-tuple-element.30, f32[128,512]{1,0:T(8,128)S(1)} %slice.165, f32[128,128]{0,1:T(8,128)} %bitcast.69, f32[128,128]{0,1:T(8,128)} %copy-done.5, f32[128,128]{0,1:T(8,128)S(1)} %bitcast.60), kind=kOutput, calls=%fused_computation.50 | convolution fusion | flops 403111936 | bytes 1245184 | tf_op jit(solution)/shard_map/dot_general | solution.py:350
  220.1 0.0 copy-done.10
  220.1 0.0 copy-done.4
  220.1 0.2 compare_reduce_fusion
  220.3 0.4 convolution_select_fusion.1
  220.8 0.0 copy-done.6
  220.8 0.0 copy-done.7
  220.8 0.4 fusion.35
  221.2 0.4 convolution_subtract_fusion.1
  221.7 2.3 fusion.13
  224.0 0.9 maximum_maximum_fusion.7
  225.0 2.8 %fusion.11 = f32[256,512]{0,1:T(8,128)} fusion(f32[256,128]{0,1:T(8,128)S(1)} %broadcast.381, f32[256,128]{0,1:T(8,128)S(1)} %get-tuple-element.44, f32[256,128]{0,1:T(8,128)S(1)} %get-tuple-element.43, f32[128,256]{1,0:T(8,128)S(1)} %get-tuple-element.38, f32[128,256]{1,0:T(8,128)S(1)} %get-tuple-element.37, ...), kind=kOutput, calls=%fused_computation.17 | convolution fusion | flops 403898368 | bytes 1639424 | tf_op jit(solution)/shard_map/dot_general | solution.py:350
  227.8 1.3 fusion.74
  229.1 1.9 fusion.20
  231.0 0.0 copy-start.1
  231.0 0.0 copy-start.2
  231.0 2.7 %fusion.75 = (f32[1,4,4,128,256]{4,3,2,1,0:T(8,128)S(1)}, f32[1,4,4,128,256]{4,3,2,1,0:T(8,128)S(1)}) fusion(f32[2,4,4,128,256]{4,3,2,1,0:T(8,128)} %get-tuple-element.12), kind=kLoop, calls=%fused_computation.148 | loop fusion | bytes 8388608 | tf_op jit(solution)/shard_map/slice | solution.py:461
  233.7 0.8 copy-done.1
  234.4 0.1 copy-done.2
  234.6 0.0 copy-start.8
  234.6 4.2 %maximum_select_fusion = f32[2048,1024]{1,0:T(8,128)S(1)} fusion(f32[2048,256]{1,0:T(8,128)S(1)} %bitcast.53, f32[2048,256]{1,0:T(8,128)S(1)} %bitcast.52, f32[2048,512]{1,0:T(8,128)S(1)} %copy-done.1, pred[2048]{0:T(1024)(128)(4,1)S(1)} %get-tuple-element.49, pred[2048,128]{1,0:T(32,128)(4,1)S(1)} %get-tuple-element.47, pred[2048,128]{1,0:T(32,128)(4,1)S(1)} %fusion.20, ...), kind=kOutput, calls=%fused_computation | convolution fusion | flops 6449528832 | bytes 18352128 | tf_op jit(solution)/shard_map/dot_general | solution.py:350
  238.8 0.0 copy-done.8
  238.8 7.1 %fusion.2 = f32[2048,512]{1,0:T(8,128)S(1)} fusion(f32[2048,1024]{1,0:T(8,128)S(1)} %maximum_select_fusion, pred[512]{0:T(512)(128)(4,1)S(1)} %fusion.72, f32[256,512]{0,1:T(8,128)S(1)} %copy-done.8, f32[256,512]{0,1:T(8,128)S(1)} %fusion.13), kind=kOutput, calls=%fused_computation.4 | convolution fusion | flops 6444810240 | bytes 13632000 | tf_op jit(solution)/shard_map/dot_general | solution.py:350
  245.9 0.0 copy-start
  245.9 2.0 copy-done
  247.9 2.3 slice.188
  250.2 1.0 fusion.28
  251.2 2.4 fusion.6
  253.6 2.3 pad_maximum_fusion
  (16 shorter events, 0.2 us)
Async XLA Ops:
  202.0 1.5 copy-start.3
  203.6 2.6 %copy-start.9 = (f32[2,2,128,128]{3,2,1,0:T(8,128)S(1)}, f32[2,2,128,128]{3,2,1,0:T(8,128)}, u32[]{:S(2)}) copy-start(f32[2,2,128,128]{3,2,1,0:T(8,128)} %param.7) | copy-start | bytes 786436
  204.8 15.3 %copy-start.10 = (s32[2,128]{1,0:T(2,128)S(1)}, s32[2,128]{1,0:T(2,128)}, u32[]{:S(2)}) copy-start(s32[2,128]{1,0:T(2,128)} %piv_ref.1) | copy-start | bytes 3076
  207.0 4.0 %copy-start.5 = (f32[128,128]{0,1:T(8,128)}, f32[128,128]{0,1:T(8,128)S(1)}, u32[]{:S(2)}) copy-start(f32[128,128]{0,1:T(8,128)S(1)} %bitcast_negate_fusion.1) | copy-start | bytes 196612
  214.1 6.7 %copy-start.6 = (f32[128,128]{0,1:T(8,128)S(1)}, f32[128,128]{0,1:T(8,128)}, u32[]{:S(2)}) copy-start(f32[128,128]{0,1:T(8,128)} %copy-done.5) | copy-start | bytes 196612
  214.1 6.7 %copy-start.7 = (f32[1,1,128,128]{2,3,1,0:T(8,128)S(1)}, f32[1,1,128,128]{2,3,1,0:T(8,128)}, u32[]{:S(2)}) copy-start(f32[1,1,128,128]{2,3,1,0:T(8,128)} %copy.19) | copy-start | bytes 196612
  215.5 4.6 %copy-start.4 = (f32[256,256]{0,1:T(8,128)}, f32[256,256]{0,1:T(8,128)S(1)}, u32[]{:S(2)}) copy-start(f32[256,256]{0,1:T(8,128)S(1)} %fusion.73) | copy-start | bytes 786436
  231.0 3.5 %copy-start.1 = (f32[2048,512]{1,0:T(8,128)S(1)}, f32[2048,512]{1,0:T(8,128)}, u32[]{:S(2)}) copy-start(f32[2048,512]{1,0:T(8,128)} %get-tuple-element.11) | copy-start | bytes 12582916
  231.0 3.6 %copy-start.2 = (f32[128,1024]{1,0:T(8,128)S(1)}, f32[128,1024]{1,0:T(8,128)}, u32[]{:S(2)}) copy-start(f32[128,1024]{1,0:T(8,128)} %get-tuple-element.25) | copy-start | bytes 1572868
  234.6 4.2 %copy-start.8 = (f32[256,512]{0,1:T(8,128)S(1)}, f32[256,512]{0,1:T(8,128)}, u32[]{:S(2)}) copy-start(f32[256,512]{0,1:T(8,128)} %fusion.11) | copy-start | bytes 1572868
  245.9 2.0 copy-start

commit v2 on v1

--- a/solution.py
+++ b/solution.py
@@ -16,8 +16,8 @@
 def comm_kernel(
     dims, idx_ref, piv_ref, lab_ref, asm_hbm,
     m_hbm, ag_hbm, fin_hbm, wfin_hbm,
-    asm, sendb, recvb, labs, mat, pb, ag, pk, rb, fin, wfin, place,
-    out_sem, lab_s, lab_r, a_s, a_r, sc_s, sc_r, rs_s, rs_r, t_s, t_r, y_s, y_r, wb_s, wb_r, wy_s, wy_r,
+    asm, sendb, mid, recvb, labs, mat, pb, ag, pk, rb, fin, wfin, place,
+    out_sem, lab_s, lab_r, a_s, a_r, b_s, b_r, sc_s, sc_r, rs_s, rs_r, t_s, t_r, y_s, y_r, wb_s, wb_r, wy_s, wy_r,
     g1_s, g1_r, g2_s, g2_r,
 ):
     rows_n, nx, nz, cap, row_tiles = dims
@@ -62,24 +62,88 @@
     labs[me_c] = lab_ref[...]
     load.wait()
 
-    def a_copy(d):
-        return remote(sendb.at[d], recvb.at[me_c], a_s.at[d], a_r.at[me_c], me_r, d)
-
-    for r in range(cap):
-        recvb[me_c, r] = asm[idx_ref[me_c * cap + r]]
-
-    def pack(k, c):
-        d = (me_c + k) % cols_n
+    def first_hop(c, d):
+        dx, dz = d // nz, d % nz
+        if c == 0:
+            return remote(sendb.at[0, d], mid.at[0, me_x * nz + dz], a_s.at[0, d], b_r.at[0, me_x * nz + dz],
+                          me_r, dx * nz + me_z)
+        return remote(sendb.at[1, d], mid.at[1, dx * nz + me_z], a_s.at[1, d], b_r.at[1, dx * nz + me_z],
+                      me_r, me_x * nz + dz)
+
+    def direct(c, d):
+        return remote(sendb.at[c, d], recvb.at[c, me_c], a_s.at[c, d], a_r.at[c, me_c], me_r, d)
+
+    def relay_in(c, dx, dz):
+        if c == 0:
+            sx = (me_x + nx - dx) % nx
+            at = sx * nz + (me_z + dz) % nz
+            return remote(sendb.at[0, at], mid.at[0, at], b_s.at[0, at], b_r.at[0, at], me_r, sx * nz + me_z)
+        sz = (me_z + nz - dz) % nz
+        at = (me_x + dx) % nx * nz + sz
+        return remote(sendb.at[1, at], mid.at[1, at], b_s.at[1, at], b_r.at[1, at], me_r, me_x * nz + sz)
+
+    def relay_out(c, dx, dz):
+        if c == 0:
+            sx = (me_x + nx - dx) % nx
+            tz = (me_z + dz) % nz
+            at = sx * nz + tz
+            src = sx * nz + me_z
+            return remote(mid.at[0, at], recvb.at[0, src], b_s.at[0, at], a_r.at[0, src], me_r, me_x * nz + tz)
+        sz = (me_z + nz - dz) % nz
+        tx = (me_x + dx) % nx
+        at = tx * nz + sz
+        src = me_x * nz + sz
+        return remote(mid.at[1, at], recvb.at[1, src], b_s.at[1, at], a_r.at[1, src], me_r, tx * nz + me_z)
+
+    def offset(k):
+        return k % (nx - 1) + 1, k // (nx - 1) + 1
+
+    def peer(dx, dz):
+        return (me_x + dx) % nx * nz + (me_z + dz) % nz
+
+    def pack_to(dst, d, e):
         for r in range(cap):
-            sendb[d, r] = asm[idx_ref[d * cap + r]]
-
-        @pl.when(k > 1)
-        def _():
-            a_copy((me_c + k - 1) % cols_n).start()
-        return c
-
-    lax.fori_loop(1, cols_n, pack, 0)
-    a_copy((me_c + cols_n - 1) % cols_n).start()
+            t = idx_ref[d * cap + r]
+            for c in range(2):
+                dst[c, e, r] = asm[t, c]
+
+    def pack(k, c0):
+        d = peer(*offset(k))
+        pack_to(sendb, d, d)
+
+        @pl.when(k > 0)
+        def _():
+            p = peer(*offset(jnp.maximum(k - 1, 0)))
+            first_hop(0, p).start()
+            first_hop(1, p).start()
+        return c0
+
+    relays = (nx - 1) * (nz - 1)
+    lax.fori_loop(0, relays, pack, 0)
+    axis_peers = [(dx, 0) for dx in range(1, nx)] + [(0, dz) for dz in range(1, nz)]
+    for n, (dx, dz) in enumerate(axis_peers):
+        d = peer(dx, dz)
+        pack_to(sendb, d, d)
+        if n == 0:
+            p = peer(*offset(relays - 1))
+            first_hop(0, p).start()
+            first_hop(1, p).start()
+        else:
+            p = peer(*axis_peers[n - 1])
+            direct(0, p).start()
+            direct(1, p).start()
+    pack_to(recvb, me_c, me_c)
+    direct(0, peer(*axis_peers[-1])).start()
+    direct(1, peer(*axis_peers[-1])).start()
+
+    def relay(k, c0):
+        dx, dz = offset(k)
+        for c in range(2):
+            relay_in(c, dx, dz).wait_recv()
+            relay_out(c, dx, dz).start()
+        return c0
+
+    lax.fori_loop(0, relays, relay, 0)
 
     def lab_wait(k, c):
         s = (me_c + k) % cols_n
@@ -101,7 +165,8 @@
 
     def a_wait(k, c):
         s = (me_c + k) % cols_n
-        remote(sendb.at[s], recvb.at[s], a_s.at[s], a_r.at[s], me_r, s).wait_recv()
+        for h in range(2):
+            remote(sendb.at[h, s], recvb.at[h, s], a_s.at[h, s], a_r.at[h, s], me_r, s).wait_recv()
         return c
 
     lax.fori_loop(1, cols_n, a_wait, 0)
@@ -112,8 +177,8 @@
             at = place[i * CBLK + m]
             s = at // cap
             r = at - s * cap
-            re = recvb[s, r, 0]
-            im = recvb[s, r, 1]
+            re = recvb[0, s, r]
+            im = recvb[1, s, r]
             mat[rows, m * NB:(m + 1) * NB] = re
             mat[rows, (CBLK + m) * NB:(CBLK + m + 1) * NB] = im
             if m == 0:
@@ -301,10 +366,18 @@
     def sent_col(k, c):
         d = (me_c + k) % cols_n
         lab_copy(d).wait_send()
-        a_copy(d).wait_send()
+        direct(0, d).wait_send()
+        direct(1, d).wait_send()
         return c
 
     lax.fori_loop(1, cols_n, sent_col, 0)
+
+    def sent_relay(k, c0):
+        for c in range(2):
+            relay_out(c, *offset(k)).wait_send()
+        return c0
+
+    lax.fori_loop(0, relays, sent_relay, 0)
 
     def sent_row(k, c):
         d = (me_r + k) % rows_n
@@ -388,8 +461,9 @@
         out_specs=(hbm, hbm, hbm, hbm),
         scratch_shapes=[
             pltpu.VMEM((slots, 2, NB, NB), f32),
-            pltpu.VMEM((cols_n, cap, 2, NB, NB), f32),
-            pltpu.VMEM((cols_n, cap, 2, NB, NB), f32),
+            pltpu.VMEM((2, cols_n, cap, NB, NB), f32),
+            pltpu.VMEM((2, cols_n, cap, NB, NB), f32),
+            pltpu.VMEM((2, cols_n, cap, NB, NB), f32),
             pltpu.VMEM((cols_n, 8, 128), jnp.int32),
             pltpu.VMEM((rows, wide), f32),
             pltpu.VMEM((row_tiles, NB, 2 * NB), f32),
@@ -401,7 +475,8 @@
             pltpu.SMEM((slots,), jnp.int32),
             dma((5,)),
             dma((cols_n,)), dma((cols_n,)),
-            dma((cols_n,)), dma((cols_n,)),
+            dma((2, cols_n)), dma((2, cols_n)),
+            dma((2, cols_n)), dma((2, cols_n)),
             dma((cols_n,)), dma((2,)),
             dma((rows_n,)), dma((rows_n,)),
             dma((rows_n,)), dma((2,)),

time: 258 us -> 206 us (0.80)
  Pallas kernels: 199 us -> 146 us
    pallas_call x1, Pallas kernels: 199 us -> 146 us  [per_device(): pl.pallas_call(functools.partial(comm_kernel, dims), out_shape=(jax.Shape...]
where the time goes in v2:
time: 206 us; the launch traced here: 203 us
  Pallas kernels  146 us (71%)
  matrix products  24.1 us (12%)
  local copies, waits for them, and re-layouts  16.7 us (8%)
  other arithmetic  16.2 us (8%)
    pallas_call x1, Pallas kernels, per_device(): pl.pallas_call(functools.partial(comm_kernel, dims), out_shape=(jax.Shape...  146 us
    dot_general x10, matrix products, dot(): return jnp.dot(a, b, precision=HI, preferred_element_type=jnp.float32)  24.1 us
    unnamed x26, local copies, waits for them, and re-layouts  7.15 us
    another operation x2, other arithmetic, per_device(): return jnp.stack([out[:, :CBLK * NB], out[:, CBLK * NB:]])  4.69 us

profile of v2, /device:TPU:20, one launch (start us, length us, event | category | flops | bytes accessed | tf_op | source)
XLA Modules:
  0.0 203.2 jit_solution(1117233988223784179)
XLA Ops:
  0.0 0.7 fusion.71
  0.7 0.7 and_select_fusion.2
  1.3 0.2 convert_reduce_fusion
  1.5 0.7 fusion.62
  2.2 0.6 select_reduce_fusion
  2.8 0.6 broadcast_in_dim.116.lab_ref
  3.4 145.8 %exchange.1 = (f32[2048,512]{1,0:T(8,128)}, f32[2,4,4,128,256]{4,3,2,1,0:T(8,128)}, f32[8,64,512]{2,1,0:T(8,128)}, f32[2,8,64,256]{3,2,1,0:T(8,128)}) custom-call(s32[128]{0:T(128)} %get-tuple-element.16.idx_ref, s32[2,128]{1,0:T(2,128)} %piv_ref.1, s32[8,128]{1,0:T(8,128)} %broadcast_in_dim.116.lab_ref, f32[32,2,128,128]{3,2,1,0:T(8,128)} %bitcast.54), custom_call_target="tpu_custom_call" | custom-call | tf_op jit(solution)/shard_map/exchange/pallas_call | solution.py:452
  149.2 0.0 copy-start.3
  149.2 1.4 fusion.76
  150.7 0.1 copy-done.3
  150.8 0.1 copy.12
  150.8 0.0 copy-start.9
  150.9 0.2 pad_maximum_fusion.2
  151.1 1.0 slice_bitcast_fusion.3
  152.1 0.0 copy-start.10
  152.1 0.7 fusion.77
  152.8 0.7 slice_negate_fusion.2
  153.4 0.0 copy-done.9
  153.4 0.7 fusion.80
  154.1 0.1 copy.20
  154.3 0.0 copy-start.5
  154.3 1.6 copy.19
  155.8 2.4 %fusion.29 = f32[256,256]{1,0:T(8,128)} fusion(f32[128,128]{1,0:T(8,128)} %get-tuple-element.32, f32[128,128]{1,0:T(8,128)} %get-tuple-element.31, f32[128,256]{1,0:T(8,128)} %get-tuple-element.28, f32[128,128]{0,1:T(8,128)} %bitcast.67, f32[128,128]{0,1:T(8,128)S(1)} %bitcast_negate_fusion.1, f32[128,128]{0,1:T(8,128)S(1)} %bitcast.58), kind=kOutput, calls=%fused_computation.55 | convolution fusion | flops 201654272 | bytes 720896 | tf_op jit(solution)/shard_map/dot_general | solution.py:423
  158.2 0.0 copy-done.5
  158.2 0.9 copy.22
  159.1 0.6 bitcast_negate_fusion
  159.8 1.6 copy.21
  161.3 0.0 copy-start.6
  161.3 0.0 copy-start.7
  161.3 1.4 fusion.73
  162.8 0.0 copy-start.4
  162.8 1.0 maximum_maximum_fusion.6
  163.8 0.8 fusion.78
  164.6 2.7 %fusion.27 = f32[256,512]{0,1:T(8,128)} fusion(f32[128,256]{1,0:T(8,128)S(1)} %get-tuple-element.29, f32[128,256]{1,0:T(8,128)S(1)} %get-tuple-element.30, f32[128,512]{1,0:T(8,128)S(1)} %slice.165, f32[128,128]{0,1:T(8,128)} %bitcast.69, f32[128,128]{0,1:T(8,128)} %copy-done.5, f32[128,128]{0,1:T(8,128)S(1)} %bitcast.60), kind=kOutput, calls=%fused_computation.50 | convolution fusion | flops 403111936 | bytes 1245184 | tf_op jit(solution)/shard_map/dot_general | solution.py:423
  167.4 0.0 copy-done.10
  167.4 0.0 copy-done.4
  167.4 0.2 compare_reduce_fusion
  167.6 0.4 convolution_select_fusion.1
  168.0 0.0 copy-done.6
  168.0 0.0 copy-done.7
  168.0 0.4 fusion.35
  168.4 0.4 convolution_subtract_fusion.1
  168.9 2.3 %fusion.13 = f32[256,512]{0,1:T(8,128)S(1)} fusion(f32[256,512]{0,1:T(8,128)} %fusion.27, f32[256,256]{0,1:T(8,128)} %copy-done.4, f32[256,128]{0,1:T(8,128)S(1)} %broadcast.381, f32[256,128]{0,1:T(8,128)} %get-tuple-element.56, f32[256,128]{0,1:T(8,128)} %get-tuple-element.57, f32[256,128]{0,1:T(8,128)} %get-tuple-element.34, ...), kind=kOutput, calls=%fused_computation.21 | convolution fusion | flops 404226048 | bytes 2491392 | tf_op jit(solution)/shard_map/dot_general | solution.py:423
  171.3 0.9 maximum_maximum_fusion.7
  172.2 2.8 %fusion.11 = f32[256,512]{0,1:T(8,128)} fusion(f32[256,128]{0,1:T(8,128)S(1)} %broadcast.381, f32[256,128]{0,1:T(8,128)S(1)} %get-tuple-element.44, f32[256,128]{0,1:T(8,128)S(1)} %get-tuple-element.43, f32[128,256]{1,0:T(8,128)S(1)} %get-tuple-element.38, f32[128,256]{1,0:T(8,128)S(1)} %get-tuple-element.37, ...), kind=kOutput, calls=%fused_computation.17 | convolution fusion | flops 403898368 | bytes 1639424 | tf_op jit(solution)/shard_map/dot_general | solution.py:423
  175.0 1.3 fusion.74
  176.3 1.9 fusion.20
  178.2 0.0 copy-start.1
  178.3 0.0 copy-start.2
  178.3 2.7 %fusion.75 = (f32[1,4,4,128,256]{4,3,2,1,0:T(8,128)S(1)}, f32[1,4,4,128,256]{4,3,2,1,0:T(8,128)S(1)}) fusion(f32[2,4,4,128,256]{4,3,2,1,0:T(8,128)} %get-tuple-element.12), kind=kLoop, calls=%fused_computation.148 | loop fusion | bytes 8388608 | tf_op jit(solution)/shard_map/slice | solution.py:536
  180.9 0.8 copy-done.1
  181.7 0.1 copy-done.2
  181.8 0.0 copy-start.8
  181.8 4.2 %maximum_select_fusion = f32[2048,1024]{1,0:T(8,128)S(1)} fusion(f32[2048,256]{1,0:T(8,128)S(1)} %bitcast.53, f32[2048,256]{1,0:T(8,128)S(1)} %bitcast.52, f32[2048,512]{1,0:T(8,128)S(1)} %copy-done.1, pred[2048]{0:T(1024)(128)(4,1)S(1)} %get-tuple-element.49, pred[2048,128]{1,0:T(32,128)(4,1)S(1)} %get-tuple-element.47, pred[2048,128]{1,0:T(32,128)(4,1)S(1)} %fusion.20, ...), kind=kOutput, calls=%fused_computation | convolution fusion | flops 6449528832 | bytes 18352128 | tf_op jit(solution)/shard_map/dot_general | solution.py:423
  186.0 0.0 copy-done.8
  186.0 7.1 %fusion.2 = f32[2048,512]{1,0:T(8,128)S(1)} fusion(f32[2048,1024]{1,0:T(8,128)S(1)} %maximum_select_fusion, pred[512]{0:T(512)(128)(4,1)S(1)} %fusion.72, f32[256,512]{0,1:T(8,128)S(1)} %copy-done.8, f32[256,512]{0,1:T(8,128)S(1)} %fusion.13), kind=kOutput, calls=%fused_computation.4 | convolution fusion | flops 6444810240 | bytes 13632000 | tf_op jit(solution)/shard_map/dot_general | solution.py:423
  193.1 0.0 copy-start
  193.1 2.0 copy-done
  195.1 2.3 %slice.188 = f32[1920,512]{1,0:T(8,128)} slice(f32[2048,512]{1,0:T(8,128)S(1)} %fusion.2), slice={[128:2048], [0:512]} | slice | bytes 7864320 | tf_op jit(solution)/shard_map/slice | solution.py:541
  197.4 1.0 fusion.28
  198.5 2.4 %fusion.6 = (f32[1,2048,256]{2,1,0:T(8,128)S(1)}, f32[1,2048,256]{2,1,0:T(8,128)S(1)}) fusion(f32[128,512]{1,0:T(8,128)S(1)} %fusion.28, f32[1920,512]{1,0:T(8,128)} %slice.188), kind=kLoop, calls=%fused_computation.9 | loop fusion | flops 1048576 | bytes 8388608 | tf_op jit(solution)/shard_map/stack | solution.py:542
  200.9 2.3 %pad_maximum_fusion = f32[2,2048,256]{2,1,0:T(8,128)} fusion(f32[1,2048,256]{2,1,0:T(8,128)S(1)} %get-tuple-element.20, f32[1,2048,256]{2,1,0:T(8,128)S(1)} %get-tuple-element.19), kind=kLoop, calls=%fused_computation.7 | loop fusion | flops 1048576 | bytes 8388608 | tf_op jit(solution)/shard_map/stack | solution.py:542
  (16 shorter events, 0.2 us)
Async XLA Ops:
  149.2 1.5 copy-start.3
  150.8 2.6 %copy-start.9 = (f32[2,2,128,128]{3,2,1,0:T(8,128)S(1)}, f32[2,2,128,128]{3,2,1,0:T(8,128)}, u32[]{:S(2)}) copy-start(f32[2,2,128,128]{3,2,1,0:T(8,128)} %param.7) | copy-start | bytes 786436
  152.1 15.3 %copy-start.10 = (s32[2,128]{1,0:T(2,128)S(1)}, s32[2,128]{1,0:T(2,128)}, u32[]{:S(2)}) copy-start(s32[2,128]{1,0:T(2,128)} %piv_ref.1) | copy-start | bytes 3076
  154.3 4.0 %copy-start.5 = (f32[128,128]{0,1:T(8,128)}, f32[128,128]{0,1:T(8,128)S(1)}, u32[]{:S(2)}) copy-start(f32[128,128]{0,1:T(8,128)S(1)} %bitcast_negate_fusion.1) | copy-start | bytes 196612
  161.3 6.7 %copy-start.6 = (f32[128,128]{0,1:T(8,128)S(1)}, f32[128,128]{0,1:T(8,128)}, u32[]{:S(2)}) copy-start(f32[128,128]{0,1:T(8,128)} %copy-done.5) | copy-start | bytes 196612
  161.3 6.7 %copy-start.7 = (f32[1,1,128,128]{2,3,1,0:T(8,128)S(1)}, f32[1,1,128,128]{2,3,1,0:T(8,128)}, u32[]{:S(2)}) copy-start(f32[1,1,128,128]{2,3,1,0:T(8,128)} %copy.19) | copy-start | bytes 196612
  162.8 4.6 %copy-start.4 = (f32[256,256]{0,1:T(8,128)}, f32[256,256]{0,1:T(8,128)S(1)}, u32[]{:S(2)}) copy-start(f32[256,256]{0,1:T(8,128)S(1)} %fusion.73) | copy-start | bytes 786436
  178.2 3.5 %copy-start.1 = (f32[2048,512]{1,0:T(8,128)S(1)}, f32[2048,512]{1,0:T(8,128)}, u32[]{:S(2)}) copy-start(f32[2048,512]{1,0:T(8,128)} %get-tuple-element.11) | copy-start | bytes 12582916
  178.3 3.6 %copy-start.2 = (f32[128,1024]{1,0:T(8,128)S(1)}, f32[128,1024]{1,0:T(8,128)}, u32[]{:S(2)}) copy-start(f32[128,1024]{1,0:T(8,128)} %get-tuple-element.25) | copy-start | bytes 1572868
  181.8 4.2 %copy-start.8 = (f32[256,512]{0,1:T(8,128)S(1)}, f32[256,512]{0,1:T(8,128)}, u32[]{:S(2)}) copy-start(f32[256,512]{0,1:T(8,128)} %fusion.11) | copy-start | bytes 1572868
  193.1 2.0 copy-start

commit v3 on v2

--- a/solution.py
+++ b/solution.py
@@ -227,7 +227,7 @@
 
     def t_copy(s, d):
         rows = pl.ds(pl.multiple_of(d * sl, sl), sl)
-        return remote(mat.at[rows, :], fin.at[d, pl.ds((2 + s) * sl, sl), :], t_s.at[d], t_r.at[s], d, me_c)
+        return remote(mat.at[rows, :], fin.at[2 + s, rows, :], t_s.at[d], t_r.at[s], d, me_c)
 
     for s in range(2):
         @pl.when(me_r == s)
@@ -236,7 +236,7 @@
                 t_copy(s, (s + k) % rows_n).start()
                 return c
             lax.fori_loop(1, rows_n, go, 0)
-            fin[s, (2 + s) * sl:(3 + s) * sl, :] = mat[s * sl:(s + 1) * sl, :]
+            fin[2 + s, s * sl:(s + 1) * sl, :] = mat[s * sl:(s + 1) * sl, :]
 
     def rs_wait(k, c):
         s = (me_r + k) % rows_n
@@ -249,15 +249,19 @@
     def add(k, acc):
         return acc + rb[(me_r + k) % rows_n]
 
-    fin[me_r, 0:2 * sl, :] = lax.fori_loop(1, rows_n, add, total)
+    total = lax.fori_loop(1, rows_n, add, total)
+    mine_rows = pl.ds(pl.multiple_of(me_r * sl, sl), sl)
+    fin[0, mine_rows, :] = total[:sl]
+    fin[1, mine_rows, :] = total[sl:]
     for s in range(2):
         @pl.when(me_r != s)
         def _():
-            part = fin.at[me_r, pl.ds((2 + s) * sl, sl), :]
+            part = fin.at[2 + s, mine_rows, :]
             remote(part, part, t_s.at[s], t_r.at[s], s, me_c).wait_recv()
 
     def y_copy(d):
-        return remote(fin.at[me_r], fin.at[me_r], y_s.at[d], y_r.at[me_r], d, me_c)
+        part = fin.at[:, mine_rows, :]
+        return remote(part, part, y_s.at[d], y_r.at[me_r], d, me_c)
 
     def y_start(k, c):
         y_copy((me_r + k) % rows_n).start()
@@ -266,13 +270,14 @@
     lax.fori_loop(1, rows_n, y_start, 0)
 
     def wb_copy(b, d):
-        return remote(wfin.at[b, me_r], wfin.at[b, me_r], wb_s.at[d], wb_r.at[b], me_r, d)
+        part = wfin.at[b, :, mine_rows, :]
+        return remote(part, part, wb_s.at[d], wb_r.at[b], me_r, d)
 
     for b in range(2):
         @pl.when(me_c == b)
         def _():
-            wfin[b, me_r, :, 0:NB] = fin[me_r, :, 0:NB]
-            wfin[b, me_r, :, NB:2 * NB] = fin[me_r, :, CBLK * NB:(CBLK + 1) * NB]
+            wfin[b, :, mine_rows, 0:NB] = fin[:, mine_rows, 0:NB]
+            wfin[b, :, mine_rows, NB:2 * NB] = fin[:, mine_rows, CBLK * NB:(CBLK + 1) * NB]
 
             def go(k, c):
                 wb_copy(b, (b + k) % cols_n).start()
@@ -312,11 +317,11 @@
     for b in range(2):
         @pl.when(me_c != b)
         def _():
-            part = wfin.at[b, me_r]
+            part = wfin.at[b, :, mine_rows, :]
             remote(part, part, wb_s.at[b], wb_r.at[b], me_r, b).wait_recv()
 
     def wy_copy(d):
-        part = wfin.at[:, me_r]
+        part = wfin.at[:, :, mine_rows, :]
         return remote(part, part, wy_s.at[d], wy_r.at[me_r], d, me_c)
 
     def wy_start(k, c):
@@ -340,9 +345,10 @@
 
     def y_wait(k, c):
         s = (me_r + k) % rows_n
-        part = fin.at[s]
+        rows = pl.ds(pl.multiple_of(s * sl, sl), sl)
+        part = fin.at[:, rows, :]
         remote(part, part, y_s.at[s], y_r.at[s], s, me_c).wait_recv()
-        part = wfin.at[:, s]
+        part = wfin.at[:, :, rows, :]
         remote(part, part, wy_s.at[s], wy_r.at[s], s, me_c).wait_recv()
         return c
 
@@ -415,12 +421,109 @@
     g_out.wait()
 
 
-def cmat(re, im):
-    return jnp.concatenate([jnp.concatenate([re, im], 1), jnp.concatenate([-im, re], 1)], 0)
+def cmat(v):
+    h = v.shape[1] // 2
+    re, im = v[:, :h], v[:, h:]
+    return jnp.concatenate([v, jnp.concatenate([-im, re], 1)], 0)
 
 
 def dot(a, b):
     return jnp.dot(a, b, precision=HI, preferred_element_type=jnp.float32)
+
+
+def mm(a, b):
+    return jnp.dot(a, b, preferred_element_type=jnp.float32)
+
+
+def split(v):
+    hi = v.astype(jnp.bfloat16)
+    return hi, (v - hi.astype(jnp.float32)).astype(jnp.bfloat16)
+
+
+def finish_kernel(rows_n, tiles_step, piv_ref, inv_ref, fin_ref, wfin_ref, m_ref, g_ref, o_ref, h, h_hi, h_lo, t3, u1_ref):
+    i = pl.program_id(0)
+    my_col = lax.axis_index("pcol")
+    my_row = lax.axis_index("prow")
+    wide = m_ref.shape[1]
+    f32 = jnp.float32
+    bf16 = jnp.bfloat16
+    spots = (slice(0, NB), slice(wide // 2, wide // 2 + NB))
+
+    @pl.when(i == 0)
+    def _():
+        for s in range(2):
+            rest = jnp.concatenate([fin_ref[2 + s], wfin_ref[0, 2 + s], wfin_ref[1, 2 + s]], 1)
+            for k in range(3):
+                piece = rest.astype(bf16)
+                t3[k, s * NB:(s + 1) * NB, :] = piece
+                rest = rest - piece.astype(f32)
+        first = jnp.broadcast_to(piv_ref[0:1, :].astype(f32), (NB, NB))
+        second = jnp.broadcast_to(piv_ref[1:2, :].astype(f32), (NB, NB)).T
+        both = (first == second).astype(f32)
+        e = both.astype(bf16)
+        from_t = mm(e, t3[2, :NB, :]) + mm(e, t3[1, :NB, :]) + mm(e, t3[0, :NB, :])
+        taken = jnp.max(both, axis=1, keepdims=True) > 0
+        p1 = jnp.where(taken, from_t, jnp.concatenate([fin_ref[1], wfin_ref[0, 1], wfin_ref[1, 1]], 1))
+        i0 = jnp.concatenate([inv_ref[0, 0], inv_ref[0, 1]], 1)
+        i1 = jnp.concatenate([inv_ref[1, 0], inv_ref[1, 1]], 1)
+        c0 = cmat(fin_ref[0])
+        l0p1 = dot(p1[:, wide:wide + 2 * NB], cmat(i0))
+        u1 = p1[:, :wide] - dot(l0p1, c0)
+        c1 = cmat(u1)
+        g = dot(dot(i0, cmat(wfin_ref[1, 0])), cmat(i1))
+        h[0:2 * NB] = cmat(dot(i0, c0) - dot(g, c1))
+        h[2 * NB:] = cmat(dot(i1, c1))
+        u1_ref[...] = u1
+
+        @pl.when(my_col == 0)
+        def _():
+            ci = cmat(i0)
+            for k, lanes in enumerate(spots):
+                h[0:2 * NB, lanes] = -ci[:, k * NB:(k + 1) * NB]
+                h[2 * NB:, lanes] = jnp.zeros((2 * NB, NB), f32)
+                u1_ref[:, lanes] = l0p1[:, k * NB:(k + 1) * NB]
+
+        @pl.when(my_col == 1)
+        def _():
+            cg = cmat(g)
+            ci = cmat(i1)
+            for k, lanes in enumerate(spots):
+                h[0:2 * NB, lanes] = cg[:, k * NB:(k + 1) * NB]
+                h[2 * NB:, lanes] = -ci[:, k * NB:(k + 1) * NB]
+
+        hi, lo = split(h[...])
+        h_hi[...] = hi
+        h_lo[...] = lo
+
+    step = tiles_step * NB
+    r = lax.broadcasted_iota(jnp.int32, (step, NB), 0)
+    row = ((i * tiles_step + r // NB) * rows_n + my_row) * NB + r % NB
+    moved = row >= 2 * NB
+    hit0 = jnp.where((row == piv_ref[0:1, :]) & moved, 1.0, 0.0)
+    hit1 = jnp.where((row == piv_ref[1:2, :]) & moved, 1.0, 0.0)
+    in0 = jnp.max(hit0, axis=1, keepdims=True)
+    in1 = jnp.max(hit1, axis=1, keepdims=True)
+    s = jnp.concatenate([hit0 * (1.0 - in1), hit1], 1).astype(bf16)
+    swap = mm(s, t3[2]) + mm(s, t3[1]) + mm(s, t3[0])
+    raw = jnp.concatenate([m_ref[...], g_ref[0].reshape(step, 2 * NB), g_ref[1].reshape(step, 2 * NB)], 1)
+    z = jnp.where(in0 + in1 > 0, swap, raw)
+    hi, lo = split(z[:, wide:])
+    update = mm(hi, h_hi[...]) + (mm(hi, h_lo[...]) + mm(lo, h_hi[...]))
+    lane = lax.broadcasted_iota(jnp.int32, (step, wide), 1)
+    panel = ((lane % (wide // 2)) < NB) & (my_col < 2)
+    out = jnp.where(panel, 0.0, z[:, :wide]) - update
+    for c in range(2):
+        o_ref[c] = out[:, c * (wide // 2):(c + 1) * (wide // 2)]
+
+    @pl.when((i == 0) & (my_row == 0))
+    def _():
+        for c in range(2):
+            o_ref[c, 0:NB] = fin_ref[0, :, c * (wide // 2):(c + 1) * (wide // 2)]
+
+    @pl.when((i == 0) & (my_row == 1))
+    def _():
+        for c in range(2):
+            o_ref[c, 0:NB] = u1_ref[:, c * (wide // 2):(c + 1) * (wide // 2)]
 
 
 def per_device(dims, assembly, slot_tile, pivots, inverses):
@@ -454,8 +557,8 @@
         out_shape=(
             jax.ShapeDtypeStruct((rows, wide), f32),
             jax.ShapeDtypeStruct((2, nx, nz, NB, 2 * NB), f32),
-            jax.ShapeDtypeStruct((rows_n, 4 * sl, wide), f32),
-            jax.ShapeDtypeStruct((2, rows_n, 4 * sl, 2 * NB), f32),
+            jax.ShapeDtypeStruct((4, NB, wide), f32),
+            jax.ShapeDtypeStruct((2, 4, NB, 2 * NB), f32),
         ),
         in_specs=[smem, smem, pl.BlockSpec(memory_space=pltpu.VMEM), hbm],
         out_specs=(hbm, hbm, hbm, hbm),
@@ -470,8 +573,8 @@
             pltpu.VMEM((2, nx, nz, NB, 2 * NB), f32),
             pltpu.VMEM((rows_n, 2 * sl, wide), f32),
             pltpu.VMEM((rows_n, 2 * sl, wide), f32),
-            pltpu.VMEM((rows_n, 4 * sl, wide), f32),
-            pltpu.VMEM((2, rows_n, 4 * sl, 2 * NB), f32),
+            pltpu.VMEM((4, NB, wide), f32),
+            pltpu.VMEM((2, 4, NB, 2 * NB), f32),
             pltpu.SMEM((slots,), jnp.int32),
             dma((5,)),
             dma((cols_n,)), dma((cols_n,)),
@@ -487,59 +590,33 @@
             dma((2, n)), dma((2, n)),
         ],
         compiler_params=pltpu.CompilerParams(
-            collective_id=0, has_side_effects=True, vmem_limit_bytes=60 * 1024 * 1024),
+            collective_id=0, has_side_effects=True, vmem_limit_bytes=63 * 1024 * 1024),
         name="exchange",
     )(send_idx, pivots, labels, tiles)
 
-    my_col = lax.axis_index("pcol")
-    my_row = lax.axis_index("prow")
-    sets = fin.reshape(rows_n, 4, sl, wide).transpose(1, 0, 2, 3).reshape(4, NB, wide)
-    wsets = wfin.reshape(2, rows_n, 4, sl, 2 * NB).transpose(0, 2, 1, 3, 4).reshape(2, 4, NB, 2 * NB)
-    wall = jnp.concatenate([sets, wsets[0], wsets[1]], -1)
-    p0, p1, t0, t1 = wall[0], wall[1], wall[2], wall[3]
-    i0 = cmat(inverses[0, 0], inverses[0, 1])
-    i1 = cmat(inverses[1, 0], inverses[1, 1])
-
-    def unpack(v):
-        h = v.shape[1] // 2
-        return cmat(v[:, :h], v[:, h:])
-
-    both = (pivots[1][:, None] == pivots[0][None, :])
-    e = both.astype(f32)
-    p1 = jnp.where(jnp.any(both, 1)[:, None], dot(e, t0), p1)
-    u0 = p0[:, :wide]
-    u0b1 = p0[:, wide + 2 * NB:]
-    l0p1 = dot(p1[:, wide:wide + 2 * NB], i0)
-    u1 = p1[:, :wide] - dot(l0p1, unpack(u0))
-    g = dot(dot(i0, unpack(u0b1)), i1)
-    ru0, ru1 = unpack(u0), unpack(u1)
-    h_lo = dot(i1, ru1)
-    h_hi = dot(i0, ru0) - dot(g, ru1)
-    col = jnp.arange(wide) % (CBLK * NB) // NB * cols_n + my_col
-    is0 = col == 0
-    is1 = col == 1
-
-    def spreadc(v):
-        pad = jnp.zeros((v.shape[0], NB), f32)
-        return jnp.concatenate([v[:, :NB], pad, v[:, NB:], pad], 1)
-    h_hi = jnp.where(is0[None, :], -spreadc(i0), jnp.where(is1[None, :], spreadc(g), h_hi))
-    h_lo = jnp.where(is0[None, :], 0.0, jnp.where(is1[None, :], -spreadc(i1), h_lo))
-    h = jnp.concatenate([h_hi, h_lo], 0)
-
-    row_global = (jnp.arange(rows) // NB * rows_n + my_row) * NB + jnp.arange(rows) % NB
-    hit0 = (row_global[:, None] == pivots[0][None, :]) & (row_global >= 2 * NB)[:, None]
-    hit1 = (row_global[:, None] == pivots[1][None, :]) & (row_global >= 2 * NB)[:, None]
-    in1 = jnp.any(hit1, 1)
-    in0 = jnp.any(hit0, 1)
-    hit0 = hit0 & ~in1[:, None]
-    swap = dot(jnp.concatenate([hit0, hit1], 1).astype(f32), jnp.concatenate([t0, t1], 0))
-    raw = jnp.concatenate([m_raw, ag[0].reshape(rows, 2 * NB), ag[1].reshape(rows, 2 * NB)], 1)
-    z = jnp.where((in0 | in1)[:, None], swap, raw)
-    out = jnp.where((is0 | is1)[None, :], 0.0, z[:, :wide]) - dot(z[:, wide:], h)
-    row1 = jnp.where(is0[None, :], spreadc(l0p1), u1)
-    top = jnp.where(my_row == 0, u0, jnp.where(my_row == 1, row1, out[:NB]))
-    out = jnp.concatenate([top, out[NB:]], 0)
-    return jnp.stack([out[:, :CBLK * NB], out[:, CBLK * NB:]])
+    tiles_step = 2
+    step = tiles_step * NB
+    whole = lambda *shape: pl.BlockSpec(shape, lambda i: (0,) * len(shape))
+    return pl.pallas_call(
+        functools.partial(finish_kernel, rows_n, tiles_step),
+        grid=(row_tiles // tiles_step,),
+        out_shape=jax.ShapeDtypeStruct((2, rows, CBLK * NB), f32),
+        in_specs=[
+            whole(2, NB), whole(2, 2, NB, NB), whole(4, NB, wide), whole(2, 4, NB, 2 * NB),
+            pl.BlockSpec((step, wide), lambda i: (i, 0)),
+            pl.BlockSpec((2, tiles_step, NB, 2 * NB), lambda i: (0, i, 0, 0)),
+        ],
+        out_specs=pl.BlockSpec((2, step, CBLK * NB), lambda i: (0, i, 0)),
+        scratch_shapes=[
+            pltpu.VMEM((4 * NB, wide), f32),
+            pltpu.VMEM((4 * NB, wide), jnp.bfloat16),
+            pltpu.VMEM((4 * NB, wide), jnp.bfloat16),
+            pltpu.VMEM((3, 2 * NB, 2 * wide), jnp.bfloat16),
+            pltpu.VMEM((NB, wide), f32),
+        ],
+        compiler_params=pltpu.CompilerParams(dimension_semantics=("arbitrary",), vmem_limit_bytes=63 * 1024 * 1024),
+        name="finish",
+    )(pivots, inverses, fin, wfin, m_raw, ag.reshape(2, row_tiles, NB, 2 * NB))
 
 
 def grid_of(cols_n):

time: 206 us -> 167 us (0.81)
  matrix products: 24.1 us -> 0 us
  local copies, waits for them, and re-layouts: 16.7 us -> 0.6 us
  Pallas kernels: 146 us -> 161 us
  other arithmetic: 16.2 us -> 2.86 us
    dot_general x10 -> x0, matrix products: 24.1 us -> none  [dot(): return jnp.dot(a, b, precision=HI, preferred_element_type=jnp.float32)]
    pallas_call x0 -> x1, Pallas kernels: none -> 15.4 us  [per_device(): pl.pallas_call(functools.partial(finish_kernel, rows_n, tiles_step), grid...]
    slice x10 -> x0, local copies, waits for them, and re-layouts: 7.91 us -> none  [the longest x1 2.66 us: per_device(): ag[0].reshape(rows, 2 * NB)]
    unnamed x26 -> x0, local copies, waits for them, and re-layouts: 7.15 us -> none
    another operation x2 -> x0, other arithmetic: 4.69 us -> none  [per_device(): return jnp.stack([out[:, :CBLK * NB], out[:, CBLK * NB:]])]
    concatenate x4 -> x0, other arithmetic: 2.88 us -> none  [the longest x2 1.95 us: cmat(): jnp.concatenate([jnp.concatenate([re, im], 1), jnp.concatenate([-im, re],...]
where the time goes in v3:
time: 167 us; the launch traced here: 165 us
  Pallas kernels  161 us (96%)
  other arithmetic  2.86 us (2%)
    pallas_call x1, Pallas kernels, per_device(): pl.pallas_call(functools.partial(comm_kernel, dims), out_shape=(jax.Shape...  146 us
    pallas_call x1, Pallas kernels, per_device(): pl.pallas_call(functools.partial(finish_kernel, rows_n, tiles_step), grid...  15.4 us

profile of v3, /device:TPU:20, one launch (start us, length us, event | category | flops | bytes accessed | tf_op | source)
XLA Modules:
  0.0 164.7 jit_solution(11886857762694640557)
XLA Ops:
  0.0 0.7 and_select_fusion.2
  0.7 0.7 fusion.4
  1.3 0.2 convert_reduce_fusion
  1.5 0.7 fusion.3
  2.2 0.7 select_reduce_fusion
  2.9 0.6 broadcast_in_dim.38.lab_ref
  3.5 145.8 %exchange.1 = (f32[2048,512]{1,0:T(8,128)}, f32[2,4,4,128,256]{4,3,2,1,0:T(8,128)}, f32[4,128,512]{2,1,0:T(8,128)}, f32[2,4,128,256]{3,2,1,0:T(8,128)}) custom-call(s32[128]{0:T(128)} %get-tuple-element.14.idx_ref, s32[2,128]{1,0:T(2,128)} %piv_ref.3, s32[8,128]{1,0:T(8,128)} %broadcast_in_dim.38.lab_ref, f32[32,2,128,128]{3,2,1,0:T(8,128)} %bitcast.14), custom_call_target="tpu_custom_call" | custom-call | tf_op jit(solution)/shard_map/exchange/pallas_call | solution.py:555
  149.3 15.4 %finish.1 = f32[2,2048,256]{2,1,0:T(8,128)} custom-call(s32[2,128]{1,0:T(2,128)} %piv_ref.3, f32[2,2,128,128]{3,2,1,0:T(8,128)} %inv_ref.1, f32[4,128,512]{2,1,0:T(8,128)} %get-tuple-element.9.fin_ref, f32[2,4,128,256]{3,2,1,0:T(8,128)} %get-tuple-element.10.wfin_ref, f32[2048,512]{1,0:T(8,128)} %get-tuple-element.11.m_ref, f32[2,16,128,256]{3,2,1,0:T(8,128)} %bitcast.15), custom_call_target="tpu_custom_call" | custom-call | tf_op jit(solution)/shard_map/finish/pallas_call | solution.py:600
  (1 shorter events, 0.0 us)

commit v4 on v3

--- a/solution.py
+++ b/solution.py
@@ -16,9 +16,9 @@
 def comm_kernel(
     dims, idx_ref, piv_ref, lab_ref, asm_hbm,
     m_hbm, ag_hbm, fin_hbm, wfin_hbm,
-    asm, sendb, mid, recvb, labs, mat, pb, ag, pk, rb, fin, wfin, place,
-    out_sem, lab_s, lab_r, a_s, a_r, b_s, b_r, sc_s, sc_r, rs_s, rs_r, t_s, t_r, y_s, y_r, wb_s, wb_r, wy_s, wy_r,
-    g1_s, g1_r, g2_s, g2_r,
+    asm, sendb, mid, recvb, labs, mat, pb, ag, st, pk, pr, ps, rb, fin, wfin, place,
+    out_sem, lab_s, lab_r, a_s, a_r, b_s, b_r, sx_s, sd_s, sr_s, st_r, sc_r, pk_s, pk_r, rs_s, rs_r, t_s, t_r,
+    y_s, y_r, k_s, k_r, wb_s, wb_r, g1_s, g1_r, g2_s, g2_r,
 ):
     rows_n, nx, nz, cap, row_tiles = dims
     cols_n = nx * nz
@@ -182,25 +182,85 @@
             mat[rows, m * NB:(m + 1) * NB] = re
             mat[rows, (CBLK + m) * NB:(CBLK + m + 1) * NB] = im
             if m == 0:
-                pb[i, :, 0:NB] = re
-                pb[i, :, NB:2 * NB] = im
+                pb[i // nz, i % nz, :, 0:NB] = re
+                pb[i // nz, i % nz, :, NB:2 * NB] = im
         return c
 
     lax.fori_loop(0, row_tiles, put, 0)
     m_out = pltpu.make_async_copy(mat, m_hbm, out_sem.at[0])
     m_out.start()
 
-    def sc_copy(b, d):
-        return remote(pb.at[d], ag.at[b, d // nz, d % nz], sc_s.at[d], sc_r.at[b], me_r, d)
+    lo = pl.ds(0, half)
+    hi = pl.ds(half, half)
+
+    def root(b):
+        return b // nz, b % nz
+
+    def out_x(b, dx):
+        return remote(pb.at[dx, :, lo, :], st.at[0, b, pl.ds(0, nz)], sx_s.at[0, dx], st_r.at[0, b],
+                      me_r, dx * nz + root(b)[1])
+
+    def out_z(b, dz):
+        return remote(pb.at[:, dz, hi, :], st.at[1, b, pl.ds(0, nx)], sx_s.at[1, dz], st_r.at[1, b],
+                      me_r, root(b)[0] * nz + dz)
+
+    def lo_to(b, src, ssem, dx, dz):
+        return remote(src, ag.at[b, dx, dz, lo, :], ssem, sc_r.at[0, b], me_r, dx * nz + dz)
+
+    def hi_to(b, src, ssem, dx, dz):
+        return remote(src, ag.at[b, dx, dz, hi, :], ssem, sc_r.at[1, b], me_r, dx * nz + dz)
+
+    def root_copies(b):
+        x0, z0 = root(b)
+        copies = []
+        for k in range(1, max(nx, nz)):
+            if k < nx:
+                copies.append(out_x(b, (x0 + k) % nx))
+            if k < nz:
+                copies.append(out_z(b, (z0 + k) % nz))
+        for k in range(1, nz):
+            dz = (z0 + k) % nz
+            copies.append(lo_to(b, pb.at[x0, dz, lo, :], sd_s.at[0, dz], x0, dz))
+        for k in range(1, nx):
+            dx = (x0 + k) % nx
+            copies.append(hi_to(b, pb.at[dx, z0, hi, :], sd_s.at[1, dx], dx, z0))
+        return copies
+
+    def relay_x_copies(b):
+        x0, z0 = root(b)
+        return [lo_to(b, st.at[0, b, (z0 + k) % nz], sr_s.at[0, b, k], me_x, (z0 + k) % nz) for k in range(1, nz)]
+
+    def relay_z_copies(b):
+        x0, z0 = root(b)
+        return [hi_to(b, st.at[1, b, (x0 + k) % nx], sr_s.at[1, b, k], (x0 + k) % nx, me_z) for k in range(1, nx)]
+
+    def is_relay_x(b):
+        x0, z0 = root(b)
+        return (me_z == z0) & (me_x != x0)
+
+    def is_relay_z(b):
+        x0, z0 = root(b)
+        return (me_x == x0) & (me_z != z0)
 
     for b in range(2):
         @pl.when(me_c == b)
         def _():
+            for copy in root_copies(b):
+                copy.start()
+            ag[b, root(b)[0], root(b)[1]] = pb[root(b)[0], root(b)[1]]
+
+    def t_copy(s, d):
+        rows = pl.ds(pl.multiple_of(d * sl, sl), sl)
+        return remote(mat.at[rows, :], fin.at[2 + s, rows, :], t_s.at[d], t_r.at[s], d, me_c)
+
+    for s in range(2):
+        @pl.when(me_r == s)
+        def _():
             def go(k, c):
-                sc_copy(b, (b + k) % cols_n).start()
+                t_copy(s, (s + k) % rows_n).start()
                 return c
-            lax.fori_loop(1, cols_n, go, 0)
-            ag[b, b // nz, b % nz] = pb[b]
+            lax.fori_loop(1, rows_n, go, 0)
+            fin[2 + s, s * sl:(s + 1) * sl, :] = mat[s * sl:(s + 1) * sl, :]
 
     def pick(d, c):
         def one(jj, c2):
@@ -210,47 +270,90 @@
                 mine = (tile % rows_n) == me_r
                 loc = tile // rows_n * NB + r % NB
                 row = mat[pl.ds(loc, 1), :]
-                pk[d, pl.ds(k * sl + jj, 1), :] = jnp.where(mine, row, 0.0)
+                pk[d % 2, d // 2, pl.ds(k * sl + jj, 1), :] = jnp.where(mine, row, 0.0)
             return c2
         return lax.fori_loop(0, sl, one, c)
 
     lax.fori_loop(0, rows_n, pick, 0)
-
-    def rs_copy(d):
-        return remote(pk.at[d], rb.at[me_r], rs_s.at[d], rs_r.at[me_r], d, me_c)
-
-    def rs_start(k, c):
-        rs_copy((me_r + k) % rows_n).start()
-        return c
-
-    lax.fori_loop(1, rows_n, rs_start, 0)
-
-    def t_copy(s, d):
-        rows = pl.ds(pl.multiple_of(d * sl, sl), sl)
-        return remote(mat.at[rows, :], fin.at[2 + s, rows, :], t_s.at[d], t_r.at[s], d, me_c)
-
-    for s in range(2):
-        @pl.when(me_r == s)
-        def _():
-            def go(k, c):
-                t_copy(s, (s + k) % rows_n).start()
-                return c
-            lax.fori_loop(1, rows_n, go, 0)
-            fin[2 + s, s * sl:(s + 1) * sl, :] = mat[s * sl:(s + 1) * sl, :]
-
-    def rs_wait(k, c):
-        s = (me_r + k) % rows_n
-        remote(pk.at[s], rb.at[s], rs_s.at[s], rs_r.at[s], s, me_c).wait_recv()
-        return c
-
-    lax.fori_loop(1, rows_n, rs_wait, 0)
-    total = pk[me_r]
-
-    def add(k, acc):
-        return acc + rb[(me_r + k) % rows_n]
-
-    total = lax.fori_loop(1, rows_n, add, total)
+    me_y = me_r // 2
+    me_k = me_r % 2
+    partner = me_y * 2 + 1 - me_k
+    ny = rows_n // 2
+
+    pk_copy = remote(pk.at[1 - me_k], pr, pk_s, pk_r, partner, me_c)
+    pk_copy.start()
+
+    for b in range(2):
+        x0, z0 = root(b)
+
+        @pl.when(is_relay_x(b))
+        def _():
+            part = st.at[0, b, pl.ds(0, nz)]
+            remote(part, part, sr_s.at[0, b, 0], st_r.at[0, b], me_r, b).wait_recv()
+            for copy in relay_x_copies(b):
+                copy.start()
+            ag[b, me_x, z0, 0:half] = st[0, b, z0]
+
+        @pl.when(is_relay_z(b))
+        def _():
+            part = st.at[1, b, pl.ds(0, nx)]
+            remote(part, part, sr_s.at[1, b, 0], st_r.at[1, b], me_r, b).wait_recv()
+            for copy in relay_z_copies(b):
+                copy.start()
+            ag[b, x0, me_z, half:NB] = st[1, b, x0]
+
+    remote(pr, pr, pk_s, pk_r, partner, me_c).wait_recv()
+    ps[...] = pk[me_k] + pr[...]
+
+    def rs_copy(ty):
+        return remote(ps.at[ty], rb.at[me_y], rs_s.at[ty], rs_r.at[me_y], ty * 2 + me_k, me_c)
+
+    for k in range(1, ny):
+        rs_copy((me_y + k) % ny).start()
+
+    def g1x(dx):
+        part = ag.at[:, me_x, me_z, lo, :]
+        return remote(part, part, g1_s.at[0, dx], g1_r.at[0, me_x], me_r, dx * nz + me_z)
+
+    def g1z(dz):
+        part = ag.at[:, me_x, me_z, hi, :]
+        return remote(part, part, g1_s.at[1, dz], g1_r.at[1, me_z], me_r, me_x * nz + dz)
+
+    def g2z(dz):
+        part = ag.at[:, :, me_z, lo, :]
+        return remote(part, part, g2_s.at[0, dz], g2_r.at[0, me_z], me_r, me_x * nz + dz)
+
+    def g2x(dx):
+        part = ag.at[:, me_x, :, hi, :]
+        return remote(part, part, g2_s.at[1, dx], g2_r.at[1, me_x], me_r, dx * nz + me_z)
+
+    for b in range(2):
+        x0, z0 = root(b)
+
+        @pl.when(me_z != z0)
+        def _():
+            part = ag.at[b, me_x, me_z, lo, :]
+            remote(part, part, sd_s.at[0, 0], sc_r.at[0, b], me_r, me_x * nz + z0).wait_recv()
+
+    for k in range(1, nx):
+        g1x((me_x + k) % nx).start()
+    for b in range(2):
+        x0, z0 = root(b)
+
+        @pl.when(me_x != x0)
+        def _():
+            part = ag.at[b, me_x, me_z, hi, :]
+            remote(part, part, sd_s.at[1, 0], sc_r.at[1, b], me_r, x0 * nz + me_z).wait_recv()
+
+    for k in range(1, nz):
+        g1z((me_z + k) % nz).start()
+
     mine_rows = pl.ds(pl.multiple_of(me_r * sl, sl), sl)
+    total = ps[me_y]
+    for k in range(1, ny):
+        sy = (me_y + k) % ny
+        remote(ps.at[sy], rb.at[sy], rs_s.at[sy], rs_r.at[sy], sy * 2 + me_k, me_c).wait_recv()
+        total = total + rb[sy]
     fin[0, mine_rows, :] = total[:sl]
     fin[1, mine_rows, :] = total[sl:]
     for s in range(2):
@@ -259,16 +362,6 @@
             part = fin.at[2 + s, mine_rows, :]
             remote(part, part, t_s.at[s], t_r.at[s], s, me_c).wait_recv()
 
-    def y_copy(d):
-        part = fin.at[:, mine_rows, :]
-        return remote(part, part, y_s.at[d], y_r.at[me_r], d, me_c)
-
-    def y_start(k, c):
-        y_copy((me_r + k) % rows_n).start()
-        return c
-
-    lax.fori_loop(1, rows_n, y_start, 0)
-
     def wb_copy(b, d):
         part = wfin.at[b, :, mine_rows, :]
         return remote(part, part, wb_s.at[d], wb_r.at[b], me_r, d)
@@ -284,51 +377,36 @@
                 return c
             lax.fori_loop(1, cols_n, go, 0)
 
-    for b in range(2):
-        @pl.when(me_c != b)
-        def _():
-            part = ag.at[b, me_x, me_z]
-            remote(part, part, sc_s.at[b], sc_r.at[b], me_r, b).wait_recv()
-
-    lo = pl.ds(0, half)
-    hi = pl.ds(half, half)
-
-    def g1x(dx):
-        part = ag.at[:, me_x, me_z, lo, :]
-        return remote(part, part, g1_s.at[0, dx], g1_r.at[0, me_x], me_r, dx * nz + me_z)
-
-    def g1z(dz):
-        part = ag.at[:, me_x, me_z, hi, :]
-        return remote(part, part, g1_s.at[1, dz], g1_r.at[1, me_z], me_r, me_x * nz + dz)
-
-    def g2z(dz):
-        part = ag.at[:, :, me_z, lo, :]
-        return remote(part, part, g2_s.at[0, dz], g2_r.at[0, me_z], me_r, me_x * nz + dz)
-
-    def g2x(dx):
-        part = ag.at[:, me_x, :, hi, :]
-        return remote(part, part, g2_s.at[1, dx], g2_r.at[1, me_x], me_r, dx * nz + me_z)
-
-    for k in range(1, nx):
-        g1x((me_x + k) % nx).start()
-    for k in range(1, nz):
-        g1z((me_z + k) % nz).start()
-
-    for b in range(2):
-        @pl.when(me_c != b)
-        def _():
-            part = wfin.at[b, :, mine_rows, :]
-            remote(part, part, wb_s.at[b], wb_r.at[b], me_r, b).wait_recv()
-
-    def wy_copy(d):
-        part = wfin.at[:, :, mine_rows, :]
-        return remote(part, part, wy_s.at[d], wy_r.at[me_r], d, me_c)
-
-    def wy_start(k, c):
-        wy_copy((me_r + k) % rows_n).start()
-        return c
-
-    lax.fori_loop(1, rows_n, wy_start, 0)
+    def rows_of(w, r):
+        rows = pl.ds(pl.multiple_of(r * sl, sl), sl)
+        return wfin.at[:, :, rows, :] if w else fin.at[:, rows, :]
+
+    def y_copy(w, ty):
+        part = rows_of(w, me_r)
+        return remote(part, part, y_s.at[w, ty], y_r.at[w, me_y], ty * 2 + me_k, me_c)
+
+    def k_copy(w, sy):
+        part = rows_of(w, sy * 2 + me_k)
+        return remote(part, part, k_s.at[w, sy], k_r.at[w, sy], partner, me_c)
+
+    def y_start(w):
+        for k in range(1, ny):
+            y_copy(w, (me_y + k) % ny).start()
+        k_copy(w, me_y).start()
+
+    def y_pass(w):
+        for k in range(1, ny):
+            sy = (me_y + k) % ny
+            part = rows_of(w, sy * 2 + me_k)
+            remote(part, part, y_s.at[w, sy], y_r.at[w, sy], sy * 2 + me_k, me_c).wait_recv()
+            k_copy(w, sy).start()
+
+    def y_end(w):
+        for sy in range(ny):
+            part = rows_of(w, sy * 2 + 1 - me_k)
+            remote(part, part, k_s.at[w, sy], k_r.at[w, sy], partner, me_c).wait_recv()
+
+    y_start(0)
 
     for k in range(1, nx):
         sx = (me_x + k) % nx
@@ -343,18 +421,19 @@
     for k in range(1, nx):
         g2x((me_x + k) % nx).start()
 
-    def y_wait(k, c):
-        s = (me_r + k) % rows_n
-        rows = pl.ds(pl.multiple_of(s * sl, sl), sl)
-        part = fin.at[:, rows, :]
-        remote(part, part, y_s.at[s], y_r.at[s], s, me_c).wait_recv()
-        part = wfin.at[:, :, rows, :]
-        remote(part, part, wy_s.at[s], wy_r.at[s], s, me_c).wait_recv()
-        return c
-
-    lax.fori_loop(1, rows_n, y_wait, 0)
+    for b in range(2):
+        @pl.when(me_c != b)
+        def _():
+            part = wfin.at[b, :, mine_rows, :]
+            remote(part, part, wb_s.at[b], wb_r.at[b], me_r, b).wait_recv()
+
+    y_start(1)
+    y_pass(0)
+    y_end(0)
     f_out = pltpu.make_async_copy(fin, fin_hbm, out_sem.at[1])
     f_out.start()
+    y_pass(1)
+    y_end(1)
     w_out = pltpu.make_async_copy(wfin, wfin_hbm, out_sem.at[2])
     w_out.start()
 
@@ -384,24 +463,34 @@
         return c0
 
     lax.fori_loop(0, relays, sent_relay, 0)
-
-    def sent_row(k, c):
-        d = (me_r + k) % rows_n
-        rs_copy(d).wait_send()
-        y_copy(d).wait_send()
-        wy_copy(d).wait_send()
-        return c
-
-    lax.fori_loop(1, rows_n, sent_row, 0)
+    pk_copy.wait_send()
+    for k in range(1, ny):
+        rs_copy((me_y + k) % ny).wait_send()
+    for w in range(2):
+        for k in range(1, ny):
+            y_copy(w, (me_y + k) % ny).wait_send()
+        for sy in range(ny):
+            k_copy(w, sy).wait_send()
     for b in range(2):
         @pl.when(me_c == b)
         def _():
+            for copy in root_copies(b):
+                copy.wait_send()
+
             def go(k, c):
-                d = (b + k) % cols_n
-                sc_copy(b, d).wait_send()
-                wb_copy(b, d).wait_send()
+                wb_copy(b, (b + k) % cols_n).wait_send()
                 return c
             lax.fori_loop(1, cols_n, go, 0)
+
+        @pl.when(is_relay_x(b))
+        def _():
+            for copy in relay_x_copies(b):
+                copy.wait_send()
+
+        @pl.when(is_relay_z(b))
+        def _():
+            for copy in relay_z_copies(b):
+                copy.wait_send()
 
         @pl.when(me_r == b)
         def _():
@@ -552,6 +641,7 @@
     hbm = pl.BlockSpec(memory_space=pl.ANY)
     smem = pl.BlockSpec(memory_space=pltpu.SMEM)
     n = max(nx, nz)
+    ny = rows_n // 2
     m_raw, ag, fin, wfin = pl.pallas_call(
         functools.partial(comm_kernel, dims),
         out_shape=(
@@ -569,10 +659,13 @@
             pltpu.VMEM((2, cols_n, cap, NB, NB), f32),
             pltpu.VMEM((cols_n, 8, 128), jnp.int32),
             pltpu.VMEM((rows, wide), f32),
-            pltpu.VMEM((row_tiles, NB, 2 * NB), f32),
+            pltpu.VMEM((nx, nz, NB, 2 * NB), f32),
             pltpu.VMEM((2, nx, nz, NB, 2 * NB), f32),
-            pltpu.VMEM((rows_n, 2 * sl, wide), f32),
-            pltpu.VMEM((rows_n, 2 * sl, wide), f32),
+            pltpu.VMEM((2, 2, n, NB // 2, 2 * NB), f32),
+            pltpu.VMEM((2, ny, 2 * sl, wide), f32),
+            pltpu.VMEM((ny, 2 * sl, wide), f32),
+            pltpu.VMEM((ny, 2 * sl, wide), f32),
+            pltpu.VMEM((ny, 2 * sl, wide), f32),
             pltpu.VMEM((4, NB, wide), f32),
             pltpu.VMEM((2, 4, NB, 2 * NB), f32),
             pltpu.SMEM((slots,), jnp.int32),
@@ -580,12 +673,12 @@
             dma((cols_n,)), dma((cols_n,)),
             dma((2, cols_n)), dma((2, cols_n)),
             dma((2, cols_n)), dma((2, cols_n)),
+            dma((2, n)), dma((2, n)), dma((2, 2, n)), dma((2, 2)), dma((2, 2)),
+            dma, dma,
+            dma((ny,)), dma((ny,)),
+            dma((rows_n,)), dma((2,)),
+            dma((2, ny)), dma((2, ny)), dma((2, ny)), dma((2, ny)),
             dma((cols_n,)), dma((2,)),
-            dma((rows_n,)), dma((rows_n,)),
-            dma((rows_n,)), dma((2,)),
-            dma((rows_n,)), dma((rows_n,)),
-            dma((cols_n,)), dma((2,)),
-            dma((rows_n,)), dma((rows_n,)),
             dma((2, n)), dma((2, n)),
             dma((2, n)), dma((2, n)),
         ],

time: 167 us -> 159 us (0.952); the launches traced: 165 us -> 159 us
  Pallas kernels: 161 us -> 155 us
    pallas_call x1, Pallas kernels: 146 us -> 140 us  [per_device(): pl.pallas_call(functools.partial(comm_kernel, dims), out_shape=(jax.Shape...]
where the time goes in v4:
time: 159 us
  Pallas kernels  155 us (97%)
  other arithmetic  2.86 us (2%)
    pallas_call x1, Pallas kernels, per_device(): pl.pallas_call(functools.partial(comm_kernel, dims), out_shape=(jax.Shape...  140 us
    pallas_call x1, Pallas kernels, per_device(): pl.pallas_call(functools.partial(finish_kernel, rows_n, tiles_step), grid...  15.4 us

profile of v4, /device:TPU:20, one launch (start us, length us, event | category | flops | bytes accessed | tf_op | source)
XLA Modules:
  0.0 158.7 jit_solution(6643982667982735960)
XLA Ops:
  0.0 0.7 and_select_fusion.2
  0.7 0.7 fusion.4
  1.3 0.2 convert_reduce_fusion
  1.5 0.7 fusion.3
  2.2 0.7 select_reduce_fusion
  2.9 0.6 broadcast_in_dim.38.lab_ref
  3.5 139.8 %exchange.1 = (f32[2048,512]{1,0:T(8,128)}, f32[2,4,4,128,256]{4,3,2,1,0:T(8,128)}, f32[4,128,512]{2,1,0:T(8,128)}, f32[2,4,128,256]{3,2,1,0:T(8,128)}) custom-call(s32[128]{0:T(128)} %get-tuple-element.14.idx_ref, s32[2,128]{1,0:T(2,128)} %piv_ref.3, s32[8,128]{1,0:T(8,128)} %broadcast_in_dim.38.lab_ref, f32[32,2,128,128]{3,2,1,0:T(8,128)} %bitcast.14), custom_call_target="tpu_custom_call" | custom-call | tf_op jit(solution)/shard_map/exchange/pallas_call | solution.py:645
  143.3 15.4 %finish.1 = f32[2,2048,256]{2,1,0:T(8,128)} custom-call(s32[2,128]{1,0:T(2,128)} %piv_ref.3, f32[2,2,128,128]{3,2,1,0:T(8,128)} %inv_ref.1, f32[4,128,512]{2,1,0:T(8,128)} %get-tuple-element.9.fin_ref, f32[2,4,128,256]{3,2,1,0:T(8,128)} %get-tuple-element.10.wfin_ref, f32[2048,512]{1,0:T(8,128)} %get-tuple-element.11.m_ref, f32[2,16,128,256]{3,2,1,0:T(8,128)} %bitcast.15), custom_call_target="tpu_custom_call" | custom-call | tf_op jit(solution)/shard_map/finish/pallas_call | solution.py:693
  (1 shorter events, 0.0 us)

commit v5 on v4

--- a/solution.py
+++ b/solution.py
@@ -9,14 +9,15 @@
 
 CBLK = 2
 NB = 128
+CHUNKS = 1
 MESH = pl.DeviceIdType.MESH
 HI = lax.Precision.HIGHEST
 
 
 def comm_kernel(
-    dims, idx_ref, piv_ref, lab_ref, asm_hbm,
-    m_hbm, ag_hbm, fin_hbm, wfin_hbm,
-    asm, sendb, mid, recvb, labs, mat, pb, ag, st, pk, pr, ps, rb, fin, wfin, place,
+    dims, slot_ref, piv_ref, piv_row, inv_ref, asm_hbm,
+    m_hbm, ag_hbm, hh_hbm, hl_hbm, done_hbm, tops_hbm,
+    asm, sendb, mid, recvb, labs, mat, pb, ag, st, pk, pr, ps, rb, fin, wfin, h, h_hi, h_lo, done, tops, plan, lab_ref, idx_ref, place,
     out_sem, lab_s, lab_r, a_s, a_r, b_s, b_r, sx_s, sd_s, sr_s, st_r, sc_r, pk_s, pk_r, rs_s, rs_r, t_s, t_r,
     y_s, y_r, k_s, k_r, wb_s, wb_r, g1_s, g1_r, g2_s, g2_r,
 ):
@@ -34,8 +35,28 @@
             src_ref=src, dst_ref=dst, send_sem=ssem, recv_sem=rsem,
             device_id=(row, col), device_id_type=MESH)
 
-    load = pltpu.make_async_copy(asm_hbm, asm, out_sem.at[4])
+    load = pltpu.make_async_copy(asm_hbm, asm, out_sem.at[6])
     load.start()
+
+    slots = slot_ref.shape[1]
+    ident = slot_ref[...]
+    column_tile = ident % (CBLK * cols_n)
+    target = column_tile % cols_n
+    local = ident // (CBLK * cols_n) * CBLK + column_tile // cols_n
+    across = jnp.broadcast_to(target, (slots, slots))
+    down = across.T
+    before = lax.broadcasted_iota(jnp.int32, (slots, slots), 1) < lax.broadcasted_iota(jnp.int32, (slots, slots), 0)
+    rank = jnp.sum(jnp.where((across == down) & before, 1, 0), axis=1, keepdims=True)
+    position = down[:, 0:1] * cap + rank
+    hit = position == lax.broadcasted_iota(jnp.int32, (slots, NB), 1)
+    slot_at = lax.broadcasted_iota(jnp.int32, (slots, NB), 0)
+    local_at = jnp.broadcast_to(local, (slots, slots)).T[:, 0:1]
+    order = jnp.sum(jnp.where(hit, slot_at, 0), axis=0, keepdims=True)
+    names = jnp.sum(jnp.where(hit, local_at + 1, 0), axis=0, keepdims=True) - 1
+    plan[...] = jnp.broadcast_to(order, (8, NB))
+    lab_ref[...] = jnp.broadcast_to(names, (8, NB))
+    to_smem = pltpu.make_async_copy(plan, idx_ref, out_sem.at[0])
+    to_smem.start()
 
     barrier = pltpu.get_barrier_semaphore()
 
@@ -60,6 +81,7 @@
 
     lax.fori_loop(1, cols_n, lab_start, 0)
     labs[me_c] = lab_ref[...]
+    to_smem.wait()
     load.wait()
 
     def first_hop(c, d):
@@ -103,7 +125,7 @@
 
     def pack_to(dst, d, e):
         for r in range(cap):
-            t = idx_ref[d * cap + r]
+            t = idx_ref[0, d * cap + r]
             for c in range(2):
                 dst[c, e, r] = asm[t, c]
 
@@ -190,49 +212,50 @@
     m_out = pltpu.make_async_copy(mat, m_hbm, out_sem.at[0])
     m_out.start()
 
-    lo = pl.ds(0, half)
-    hi = pl.ds(half, half)
+    piece = NB // (2 * CHUNKS)
+
+    def part_rows(kind, ch):
+        return pl.ds((kind * CHUNKS + ch) * piece, piece)
 
     def root(b):
         return b // nz, b % nz
 
-    def out_x(b, dx):
-        return remote(pb.at[dx, :, lo, :], st.at[0, b, pl.ds(0, nz)], sx_s.at[0, dx], st_r.at[0, b],
-                      me_r, dx * nz + root(b)[1])
-
-    def out_z(b, dz):
-        return remote(pb.at[:, dz, hi, :], st.at[1, b, pl.ds(0, nx)], sx_s.at[1, dz], st_r.at[1, b],
-                      me_r, root(b)[0] * nz + dz)
-
-    def lo_to(b, src, ssem, dx, dz):
-        return remote(src, ag.at[b, dx, dz, lo, :], ssem, sc_r.at[0, b], me_r, dx * nz + dz)
-
-    def hi_to(b, src, ssem, dx, dz):
-        return remote(src, ag.at[b, dx, dz, hi, :], ssem, sc_r.at[1, b], me_r, dx * nz + dz)
-
-    def root_copies(b):
+    def out_x(b, ch, dx):
+        return remote(pb.at[dx, :, part_rows(0, ch), :], st.at[0, ch, b, pl.ds(0, nz)], sx_s.at[0, ch, dx],
+                      st_r.at[0, ch, b], me_r, dx * nz + root(b)[1])
+
+    def out_z(b, ch, dz):
+        return remote(pb.at[:, dz, part_rows(1, ch), :], st.at[1, ch, b, pl.ds(0, nx)], sx_s.at[1, ch, dz],
+                      st_r.at[1, ch, b], me_r, root(b)[0] * nz + dz)
+
+    def to_tile(b, kind, ch, src, ssem, dx, dz):
+        return remote(src, ag.at[b, dx, dz, part_rows(kind, ch), :], ssem, sc_r.at[kind, ch, b], me_r, dx * nz + dz)
+
+    def root_copies(b, ch):
         x0, z0 = root(b)
         copies = []
         for k in range(1, max(nx, nz)):
             if k < nx:
-                copies.append(out_x(b, (x0 + k) % nx))
+                copies.append(out_x(b, ch, (x0 + k) % nx))
             if k < nz:
-                copies.append(out_z(b, (z0 + k) % nz))
+                copies.append(out_z(b, ch, (z0 + k) % nz))
         for k in range(1, nz):
             dz = (z0 + k) % nz
-            copies.append(lo_to(b, pb.at[x0, dz, lo, :], sd_s.at[0, dz], x0, dz))
+            copies.append(to_tile(b, 0, ch, pb.at[x0, dz, part_rows(0, ch), :], sd_s.at[0, ch, dz], x0, dz))
         for k in range(1, nx):
             dx = (x0 + k) % nx
-            copies.append(hi_to(b, pb.at[dx, z0, hi, :], sd_s.at[1, dx], dx, z0))
+            copies.append(to_tile(b, 1, ch, pb.at[dx, z0, part_rows(1, ch), :], sd_s.at[1, ch, dx], dx, z0))
         return copies
 
-    def relay_x_copies(b):
-        x0, z0 = root(b)
-        return [lo_to(b, st.at[0, b, (z0 + k) % nz], sr_s.at[0, b, k], me_x, (z0 + k) % nz) for k in range(1, nz)]
-
-    def relay_z_copies(b):
-        x0, z0 = root(b)
-        return [hi_to(b, st.at[1, b, (x0 + k) % nx], sr_s.at[1, b, k], (x0 + k) % nx, me_z) for k in range(1, nx)]
+    def relay_x_copies(b, ch):
+        z0 = root(b)[1]
+        return [to_tile(b, 0, ch, st.at[0, ch, b, (z0 + k) % nz], sr_s.at[0, ch, b, k], me_x, (z0 + k) % nz)
+                for k in range(1, nz)]
+
+    def relay_z_copies(b, ch):
+        x0 = root(b)[0]
+        return [to_tile(b, 1, ch, st.at[1, ch, b, (x0 + k) % nx], sr_s.at[1, ch, b, k], (x0 + k) % nx, me_z)
+                for k in range(1, nx)]
 
     def is_relay_x(b):
         x0, z0 = root(b)
@@ -245,9 +268,92 @@
     for b in range(2):
         @pl.when(me_c == b)
         def _():
-            for copy in root_copies(b):
-                copy.start()
+            for ch in range(CHUNKS):
+                for copy in root_copies(b, ch):
+                    copy.start()
             ag[b, root(b)[0], root(b)[1]] = pb[root(b)[0], root(b)[1]]
+
+    def pass_on(ch):
+        for b in range(2):
+            x0, z0 = root(b)
+
+            @pl.when(is_relay_x(b))
+            def _():
+                part = st.at[0, ch, b, pl.ds(0, nz)]
+                remote(part, part, sr_s.at[0, ch, b, 0], st_r.at[0, ch, b], me_r, b).wait_recv()
+                for copy in relay_x_copies(b, ch):
+                    copy.start()
+                ag[b, me_x, z0, part_rows(0, ch), :] = st[0, ch, b, z0]
+
+            @pl.when(is_relay_z(b))
+            def _():
+                part = st.at[1, ch, b, pl.ds(0, nx)]
+                remote(part, part, sr_s.at[1, ch, b, 0], st_r.at[1, ch, b], me_r, b).wait_recv()
+                for copy in relay_z_copies(b, ch):
+                    copy.start()
+                ag[b, x0, me_z, part_rows(1, ch), :] = st[1, ch, b, x0]
+
+    def g1x(ch, dx):
+        part = ag.at[:, me_x, me_z, part_rows(0, ch), :]
+        return remote(part, part, g1_s.at[0, ch, dx], g1_r.at[0, ch, me_x], me_r, dx * nz + me_z)
+
+    def g1z(ch, dz):
+        part = ag.at[:, me_x, me_z, part_rows(1, ch), :]
+        return remote(part, part, g1_s.at[1, ch, dz], g1_r.at[1, ch, me_z], me_r, me_x * nz + dz)
+
+    def g2z(ch, dz):
+        part = ag.at[:, :, me_z, part_rows(0, ch), :]
+        return remote(part, part, g2_s.at[0, ch, dz], g2_r.at[0, ch, me_z], me_r, me_x * nz + dz)
+
+    def g2x(ch, dx):
+        part = ag.at[:, me_x, :, part_rows(1, ch), :]
+        return remote(part, part, g2_s.at[1, ch, dx], g2_r.at[1, ch, me_x], me_r, dx * nz + me_z)
+
+    def gather_first(ch):
+        for b in range(2):
+            z0 = root(b)[1]
+
+            @pl.when(me_z != z0)
+            def _():
+                part = ag.at[b, me_x, me_z, part_rows(0, ch), :]
+                remote(part, part, sd_s.at[0, ch, 0], sc_r.at[0, ch, b], me_r, me_x * nz + z0).wait_recv()
+
+        for k in range(1, nx):
+            g1x(ch, (me_x + k) % nx).start()
+        for b in range(2):
+            x0 = root(b)[0]
+
+            @pl.when(me_x != x0)
+            def _():
+                part = ag.at[b, me_x, me_z, part_rows(1, ch), :]
+                remote(part, part, sd_s.at[1, ch, 0], sc_r.at[1, ch, b], me_r, x0 * nz + me_z).wait_recv()
+
+        for k in range(1, nz):
+            g1z(ch, (me_z + k) % nz).start()
+
+    def gather_second(ch):
+        for k in range(1, nx):
+            sx = (me_x + k) % nx
+            part = ag.at[:, sx, me_z, part_rows(0, ch), :]
+            remote(part, part, g1_s.at[0, ch, sx], g1_r.at[0, ch, sx], me_r, sx * nz + me_z).wait_recv()
+        for k in range(1, nz):
+            g2z(ch, (me_z + k) % nz).start()
+        for k in range(1, nz):
+            sz = (me_z + k) % nz
+            part = ag.at[:, me_x, sz, part_rows(1, ch), :]
+            remote(part, part, g1_s.at[1, ch, sz], g1_r.at[1, ch, sz], me_r, me_x * nz + sz).wait_recv()
+        for k in range(1, nx):
+            g2x(ch, (me_x + k) % nx).start()
+
+    def gather_end(ch):
+        for k in range(1, nz):
+            sz = (me_z + k) % nz
+            part = ag.at[:, :, sz, part_rows(0, ch), :]
+            remote(part, part, g2_s.at[0, ch, sz], g2_r.at[0, ch, sz], me_r, me_x * nz + sz).wait_recv()
+        for k in range(1, nx):
+            sx = (me_x + k) % nx
+            part = ag.at[:, sx, :, part_rows(1, ch), :]
+            remote(part, part, g2_s.at[1, ch, sx], g2_r.at[1, ch, sx], me_r, sx * nz + me_z).wait_recv()
 
     def t_copy(s, d):
         rows = pl.ds(pl.multiple_of(d * sl, sl), sl)
@@ -283,24 +389,7 @@
     pk_copy = remote(pk.at[1 - me_k], pr, pk_s, pk_r, partner, me_c)
     pk_copy.start()
 
-    for b in range(2):
-        x0, z0 = root(b)
-
-        @pl.when(is_relay_x(b))
-        def _():
-            part = st.at[0, b, pl.ds(0, nz)]
-            remote(part, part, sr_s.at[0, b, 0], st_r.at[0, b], me_r, b).wait_recv()
-            for copy in relay_x_copies(b):
-                copy.start()
-            ag[b, me_x, z0, 0:half] = st[0, b, z0]
-
-        @pl.when(is_relay_z(b))
-        def _():
-            part = st.at[1, b, pl.ds(0, nx)]
-            remote(part, part, sr_s.at[1, b, 0], st_r.at[1, b], me_r, b).wait_recv()
-            for copy in relay_z_copies(b):
-                copy.start()
-            ag[b, x0, me_z, half:NB] = st[1, b, x0]
+    pass_on(0)
 
     remote(pr, pr, pk_s, pk_r, partner, me_c).wait_recv()
     ps[...] = pk[me_k] + pr[...]
@@ -311,42 +400,9 @@
     for k in range(1, ny):
         rs_copy((me_y + k) % ny).start()
 
-    def g1x(dx):
-        part = ag.at[:, me_x, me_z, lo, :]
-        return remote(part, part, g1_s.at[0, dx], g1_r.at[0, me_x], me_r, dx * nz + me_z)
-
-    def g1z(dz):
-        part = ag.at[:, me_x, me_z, hi, :]
-        return remote(part, part, g1_s.at[1, dz], g1_r.at[1, me_z], me_r, me_x * nz + dz)
-
-    def g2z(dz):
-        part = ag.at[:, :, me_z, lo, :]
-        return remote(part, part, g2_s.at[0, dz], g2_r.at[0, me_z], me_r, me_x * nz + dz)
-
-    def g2x(dx):
-        part = ag.at[:, me_x, :, hi, :]
-        return remote(part, part, g2_s.at[1, dx], g2_r.at[1, me_x], me_r, dx * nz + me_z)
-
-    for b in range(2):
-        x0, z0 = root(b)
-
-        @pl.when(me_z != z0)
-        def _():
-            part = ag.at[b, me_x, me_z, lo, :]
-            remote(part, part, sd_s.at[0, 0], sc_r.at[0, b], me_r, me_x * nz + z0).wait_recv()
-
-    for k in range(1, nx):
-        g1x((me_x + k) % nx).start()
-    for b in range(2):
-        x0, z0 = root(b)
-
-        @pl.when(me_x != x0)
-        def _():
-            part = ag.at[b, me_x, me_z, hi, :]
-            remote(part, part, sd_s.at[1, 0], sc_r.at[1, b], me_r, x0 * nz + me_z).wait_recv()
-
-    for k in range(1, nz):
-        g1z((me_z + k) % nz).start()
+    gather_first(0)
+    for ch in range(1, CHUNKS):
+        pass_on(ch)
 
     mine_rows = pl.ds(pl.multiple_of(me_r * sl, sl), sl)
     total = ps[me_y]
@@ -408,18 +464,10 @@
 
     y_start(0)
 
-    for k in range(1, nx):
-        sx = (me_x + k) % nx
-        part = ag.at[:, sx, me_z, lo, :]
-        remote(part, part, g1_s.at[0, sx], g1_r.at[0, sx], me_r, sx * nz + me_z).wait_recv()
-    for k in range(1, nz):
-        g2z((me_z + k) % nz).start()
-    for k in range(1, nz):
-        sz = (me_z + k) % nz
-        part = ag.at[:, me_x, sz, hi, :]
-        remote(part, part, g1_s.at[1, sz], g1_r.at[1, sz], me_r, me_x * nz + sz).wait_recv()
-    for k in range(1, nx):
-        g2x((me_x + k) % nx).start()
+    gather_second(0)
+    for ch in range(1, CHUNKS):
+        gather_first(ch)
+        gather_second(ch)
 
     for b in range(2):
         @pl.when(me_c != b)
@@ -430,22 +478,16 @@
     y_start(1)
     y_pass(0)
     y_end(0)
-    f_out = pltpu.make_async_copy(fin, fin_hbm, out_sem.at[1])
-    f_out.start()
     y_pass(1)
     y_end(1)
-    w_out = pltpu.make_async_copy(wfin, wfin_hbm, out_sem.at[2])
-    w_out.start()
-
-    for k in range(1, nz):
-        sz = (me_z + k) % nz
-        part = ag.at[:, :, sz, lo, :]
-        remote(part, part, g2_s.at[0, sz], g2_r.at[0, sz], me_r, me_x * nz + sz).wait_recv()
-    for k in range(1, nx):
-        sx = (me_x + k) % nx
-        part = ag.at[:, sx, :, hi, :]
-        remote(part, part, g2_s.at[1, sx], g2_r.at[1, sx], me_r, sx * nz + me_z).wait_recv()
-    g_out = pltpu.make_async_copy(ag, ag_hbm, out_sem.at[3])
+    factors(piv_row, inv_ref, fin, wfin, me_c, h, h_hi, h_lo, done, tops)
+    small = [pltpu.make_async_copy(v, w, out_sem.at[1 + k]) for k, (v, w) in enumerate(
+        ((h_hi, hh_hbm), (h_lo, hl_hbm), (done, done_hbm), (tops, tops_hbm)))]
+    for copy in small:
+        copy.start()
+    for ch in range(CHUNKS):
+        gather_end(ch)
+    g_out = pltpu.make_async_copy(ag, ag_hbm, out_sem.at[5])
     g_out.start()
 
     def sent_col(k, c):
@@ -474,8 +516,9 @@
     for b in range(2):
         @pl.when(me_c == b)
         def _():
-            for copy in root_copies(b):
-                copy.wait_send()
+            for ch in range(CHUNKS):
+                for copy in root_copies(b, ch):
+                    copy.wait_send()
 
             def go(k, c):
                 wb_copy(b, (b + k) % cols_n).wait_send()
@@ -484,13 +527,15 @@
 
         @pl.when(is_relay_x(b))
         def _():
-            for copy in relay_x_copies(b):
-                copy.wait_send()
+            for ch in range(CHUNKS):
+                for copy in relay_x_copies(b, ch):
+                    copy.wait_send()
 
         @pl.when(is_relay_z(b))
         def _():
-            for copy in relay_z_copies(b):
-                copy.wait_send()
+            for ch in range(CHUNKS):
+                for copy in relay_z_copies(b, ch):
+                    copy.wait_send()
 
         @pl.when(me_r == b)
         def _():
@@ -498,15 +543,16 @@
                 t_copy(b, (b + k) % rows_n).wait_send()
                 return c
             lax.fori_loop(1, rows_n, go, 0)
-    for k in range(1, nx):
-        g1x((me_x + k) % nx).wait_send()
-        g2x((me_x + k) % nx).wait_send()
-    for k in range(1, nz):
-        g1z((me_z + k) % nz).wait_send()
-        g2z((me_z + k) % nz).wait_send()
+    for ch in range(CHUNKS):
+        for k in range(1, nx):
+            g1x(ch, (me_x + k) % nx).wait_send()
+            g2x(ch, (me_x + k) % nx).wait_send()
+        for k in range(1, nz):
+            g1z(ch, (me_z + k) % nz).wait_send()
+            g2z(ch, (me_z + k) % nz).wait_send()
     m_out.wait()
-    f_out.wait()
-    w_out.wait()
+    for copy in small:
+        copy.wait()
     g_out.wait()
 
 
@@ -529,61 +575,70 @@
     return hi, (v - hi.astype(jnp.float32)).astype(jnp.bfloat16)
 
 
-def finish_kernel(rows_n, tiles_step, piv_ref, inv_ref, fin_ref, wfin_ref, m_ref, g_ref, o_ref, h, h_hi, h_lo, t3, u1_ref):
+def finished(own, panel, h_hi, h_lo, my_col):
+    wide = own.shape[1]
+    hi, lo = split(panel)
+    update = mm(hi, h_hi[...]) + (mm(hi, h_lo[...]) + mm(lo, h_hi[...]))
+    lane = lax.broadcasted_iota(jnp.int32, own.shape, 1)
+    first = ((lane % (wide // 2)) < NB) & (my_col < 2)
+    return jnp.where(first, 0.0, own) - update
+
+
+def factors(piv_ref, inv_ref, fin, wfin, my_col, h, h_hi, h_lo, done, tops):
+    wide = fin.shape[2]
+    f32 = jnp.float32
+    spots = (slice(0, NB), slice(wide // 2, wide // 2 + NB))
+    first = jnp.broadcast_to(piv_ref[0:1, :].astype(f32), (NB, NB))
+    second = jnp.broadcast_to(piv_ref[1:2, :].astype(f32), (NB, NB)).T
+    both = jnp.where(first == second, 1.0, 0.0)
+    from_t = dot(both, jnp.concatenate([fin[2], wfin[0, 2], wfin[1, 2]], 1))
+    taken = jnp.max(both, axis=1, keepdims=True) > 0
+    p1 = jnp.where(taken, from_t, jnp.concatenate([fin[1], wfin[0, 1], wfin[1, 1]], 1))
+    i0 = jnp.concatenate([inv_ref[0, 0], inv_ref[0, 1]], 1)
+    i1 = jnp.concatenate([inv_ref[1, 0], inv_ref[1, 1]], 1)
+    c0 = cmat(fin[0])
+    l0p1 = dot(p1[:, wide:wide + 2 * NB], cmat(i0))
+    u1 = p1[:, :wide] - dot(l0p1, c0)
+    c1 = cmat(u1)
+    g = dot(dot(i0, cmat(wfin[1, 0])), cmat(i1))
+    h[0:2 * NB] = cmat(dot(i0, c0) - dot(g, c1))
+    h[2 * NB:] = cmat(dot(i1, c1))
+    tops[0] = fin[0]
+    tops[1] = u1
+
+    @pl.when(my_col == 0)
+    def _():
+        ci = cmat(i0)
+        for k, lanes in enumerate(spots):
+            h[0:2 * NB, lanes] = -ci[:, k * NB:(k + 1) * NB]
+            h[2 * NB:, lanes] = jnp.zeros((2 * NB, NB), f32)
+            tops[1, :, lanes] = l0p1[:, k * NB:(k + 1) * NB]
+
+    @pl.when(my_col == 1)
+    def _():
+        cg = cmat(g)
+        ci = cmat(i1)
+        for k, lanes in enumerate(spots):
+            h[0:2 * NB, lanes] = cg[:, k * NB:(k + 1) * NB]
+            h[2 * NB:, lanes] = -ci[:, k * NB:(k + 1) * NB]
+
+    high, low = split(h[...])
+    h_hi[...] = high
+    h_lo[...] = low
+    rest = jnp.concatenate([fin[2], fin[3]], 0)
+    panel = jnp.concatenate([jnp.concatenate([wfin[b, 2], wfin[b, 3]], 0) for b in range(2)], 1)
+    rest = finished(rest, panel, h_hi, h_lo, my_col)
+    high, low = split(rest)
+    done[0] = high
+    done[1] = low
+
+
+def finish_kernel(rows_n, tiles_step, piv_ref, h_hi, h_lo, done, tops, m_ref, g_ref, o_ref):
     i = pl.program_id(0)
     my_col = lax.axis_index("pcol")
     my_row = lax.axis_index("prow")
     wide = m_ref.shape[1]
-    f32 = jnp.float32
     bf16 = jnp.bfloat16
-    spots = (slice(0, NB), slice(wide // 2, wide // 2 + NB))
-
-    @pl.when(i == 0)
-    def _():
-        for s in range(2):
-            rest = jnp.concatenate([fin_ref[2 + s], wfin_ref[0, 2 + s], wfin_ref[1, 2 + s]], 1)
-            for k in range(3):
-                piece = rest.astype(bf16)
-                t3[k, s * NB:(s + 1) * NB, :] = piece
-                rest = rest - piece.astype(f32)
-        first = jnp.broadcast_to(piv_ref[0:1, :].astype(f32), (NB, NB))
-        second = jnp.broadcast_to(piv_ref[1:2, :].astype(f32), (NB, NB)).T
-        both = (first == second).astype(f32)
-        e = both.astype(bf16)
-        from_t = mm(e, t3[2, :NB, :]) + mm(e, t3[1, :NB, :]) + mm(e, t3[0, :NB, :])
-        taken = jnp.max(both, axis=1, keepdims=True) > 0
-        p1 = jnp.where(taken, from_t, jnp.concatenate([fin_ref[1], wfin_ref[0, 1], wfin_ref[1, 1]], 1))
-        i0 = jnp.concatenate([inv_ref[0, 0], inv_ref[0, 1]], 1)
-        i1 = jnp.concatenate([inv_ref[1, 0], inv_ref[1, 1]], 1)
-        c0 = cmat(fin_ref[0])
-        l0p1 = dot(p1[:, wide:wide + 2 * NB], cmat(i0))
-        u1 = p1[:, :wide] - dot(l0p1, c0)
-        c1 = cmat(u1)
-        g = dot(dot(i0, cmat(wfin_ref[1, 0])), cmat(i1))
-        h[0:2 * NB] = cmat(dot(i0, c0) - dot(g, c1))
-        h[2 * NB:] = cmat(dot(i1, c1))
-        u1_ref[...] = u1
-
-        @pl.when(my_col == 0)
-        def _():
-            ci = cmat(i0)
-            for k, lanes in enumerate(spots):
-                h[0:2 * NB, lanes] = -ci[:, k * NB:(k + 1) * NB]
-                h[2 * NB:, lanes] = jnp.zeros((2 * NB, NB), f32)
-                u1_ref[:, lanes] = l0p1[:, k * NB:(k + 1) * NB]
-
-        @pl.when(my_col == 1)
-        def _():
-            cg = cmat(g)
-            ci = cmat(i1)
-            for k, lanes in enumerate(spots):
-                h[0:2 * NB, lanes] = cg[:, k * NB:(k + 1) * NB]
-                h[2 * NB:, lanes] = -ci[:, k * NB:(k + 1) * NB]
-
-        hi, lo = split(h[...])
-        h_hi[...] = hi
-        h_lo[...] = lo
-
     step = tiles_step * NB
     r = lax.broadcasted_iota(jnp.int32, (step, NB), 0)
     row = ((i * tiles_step + r // NB) * rows_n + my_row) * NB + r % NB
@@ -593,26 +648,21 @@
     in0 = jnp.max(hit0, axis=1, keepdims=True)
     in1 = jnp.max(hit1, axis=1, keepdims=True)
     s = jnp.concatenate([hit0 * (1.0 - in1), hit1], 1).astype(bf16)
-    swap = mm(s, t3[2]) + mm(s, t3[1]) + mm(s, t3[0])
-    raw = jnp.concatenate([m_ref[...], g_ref[0].reshape(step, 2 * NB), g_ref[1].reshape(step, 2 * NB)], 1)
-    z = jnp.where(in0 + in1 > 0, swap, raw)
-    hi, lo = split(z[:, wide:])
-    update = mm(hi, h_hi[...]) + (mm(hi, h_lo[...]) + mm(lo, h_hi[...]))
-    lane = lax.broadcasted_iota(jnp.int32, (step, wide), 1)
-    panel = ((lane % (wide // 2)) < NB) & (my_col < 2)
-    out = jnp.where(panel, 0.0, z[:, :wide]) - update
+    swap = mm(s, done[0]) + mm(s, done[1])
+    panel = jnp.concatenate([g_ref[0].reshape(step, 2 * NB), g_ref[1].reshape(step, 2 * NB)], 1)
+    out = jnp.where(in0 + in1 > 0, swap, finished(m_ref[...], panel, h_hi, h_lo, my_col))
     for c in range(2):
         o_ref[c] = out[:, c * (wide // 2):(c + 1) * (wide // 2)]
 
     @pl.when((i == 0) & (my_row == 0))
     def _():
         for c in range(2):
-            o_ref[c, 0:NB] = fin_ref[0, :, c * (wide // 2):(c + 1) * (wide // 2)]
+            o_ref[c, 0:NB] = tops[0, :, c * (wide // 2):(c + 1) * (wide // 2)]
 
     @pl.when((i == 0) & (my_row == 1))
     def _():
         for c in range(2):
-            o_ref[c, 0:NB] = u1_ref[:, c * (wide // 2):(c + 1) * (wide // 2)]
+            o_ref[c, 0:NB] = tops[1, :, c * (wide // 2):(c + 1) * (wide // 2)]
 
 
 def per_device(dims, assembly, slot_tile, pivots, inverses):
@@ -620,19 +670,6 @@
     cols_n = nx * nz
     tiles = assembly[0]
     slots = tiles.shape[0]
-    width_tiles = CBLK * cols_n
-    ident = slot_tile[0]
-    column_tile = ident % width_tiles
-    target = column_tile % cols_n
-    local_id = ident // width_tiles * CBLK + column_tile // cols_n
-    num = jnp.arange(slots, dtype=jnp.int32)
-    rank = jnp.sum(((target[:, None] == target[None, :]) & (num[None, :] < num[:, None])).astype(jnp.int32), axis=1)
-    position = target * cap + rank
-    hit = position[None, :] == jnp.arange(128, dtype=jnp.int32)[:, None]
-    send_idx = jnp.sum(jnp.where(hit, num[None, :], 0), axis=1)
-    labels = jnp.sum(jnp.where(hit, local_id[None, :] + 1, 0), axis=1) - 1
-    labels = jnp.broadcast_to(labels[None, :], (8, 128))
-
     sl = NB // rows_n
     rows = row_tiles * NB
     wide = 2 * CBLK * NB
@@ -640,18 +677,22 @@
     dma = pltpu.SemaphoreType.DMA
     hbm = pl.BlockSpec(memory_space=pl.ANY)
     smem = pl.BlockSpec(memory_space=pltpu.SMEM)
+    vmem = pl.BlockSpec(memory_space=pltpu.VMEM)
     n = max(nx, nz)
     ny = rows_n // 2
-    m_raw, ag, fin, wfin = pl.pallas_call(
+    bf16 = jnp.bfloat16
+    m_raw, ag, hh, hl, done, tops = pl.pallas_call(
         functools.partial(comm_kernel, dims),
         out_shape=(
             jax.ShapeDtypeStruct((rows, wide), f32),
             jax.ShapeDtypeStruct((2, nx, nz, NB, 2 * NB), f32),
-            jax.ShapeDtypeStruct((4, NB, wide), f32),
-            jax.ShapeDtypeStruct((2, 4, NB, 2 * NB), f32),
+            jax.ShapeDtypeStruct((4 * NB, wide), bf16),
+            jax.ShapeDtypeStruct((4 * NB, wide), bf16),
+            jax.ShapeDtypeStruct((2, 2 * NB, wide), bf16),
+            jax.ShapeDtypeStruct((2, NB, wide), f32),
         ),
-        in_specs=[smem, smem, pl.BlockSpec(memory_space=pltpu.VMEM), hbm],
-        out_specs=(hbm, hbm, hbm, hbm),
+        in_specs=[vmem, smem, vmem, vmem, hbm],
+        out_specs=(hbm,) * 6,
         scratch_shapes=[
             pltpu.VMEM((slots, 2, NB, NB), f32),
             pltpu.VMEM((2, cols_n, cap, NB, NB), f32),
@@ -661,31 +702,39 @@
             pltpu.VMEM((rows, wide), f32),
             pltpu.VMEM((nx, nz, NB, 2 * NB), f32),
             pltpu.VMEM((2, nx, nz, NB, 2 * NB), f32),
-            pltpu.VMEM((2, 2, n, NB // 2, 2 * NB), f32),
+            pltpu.VMEM((2, CHUNKS, 2, n, NB // (2 * CHUNKS), 2 * NB), f32),
             pltpu.VMEM((2, ny, 2 * sl, wide), f32),
             pltpu.VMEM((ny, 2 * sl, wide), f32),
             pltpu.VMEM((ny, 2 * sl, wide), f32),
             pltpu.VMEM((ny, 2 * sl, wide), f32),
             pltpu.VMEM((4, NB, wide), f32),
             pltpu.VMEM((2, 4, NB, 2 * NB), f32),
+            pltpu.VMEM((4 * NB, wide), f32),
+            pltpu.VMEM((4 * NB, wide), bf16),
+            pltpu.VMEM((4 * NB, wide), bf16),
+            pltpu.VMEM((2, 2 * NB, wide), bf16),
+            pltpu.VMEM((2, NB, wide), f32),
+            pltpu.VMEM((8, NB), jnp.int32),
+            pltpu.VMEM((8, NB), jnp.int32),
+            pltpu.SMEM((8, NB), jnp.int32),
             pltpu.SMEM((slots,), jnp.int32),
-            dma((5,)),
+            dma((7,)),
             dma((cols_n,)), dma((cols_n,)),
             dma((2, cols_n)), dma((2, cols_n)),
             dma((2, cols_n)), dma((2, cols_n)),
-            dma((2, n)), dma((2, n)), dma((2, 2, n)), dma((2, 2)), dma((2, 2)),
+            dma((2, CHUNKS, n)), dma((2, CHUNKS, n)), dma((2, CHUNKS, 2, n)), dma((2, CHUNKS, 2)), dma((2, CHUNKS, 2)),
             dma, dma,
             dma((ny,)), dma((ny,)),
             dma((rows_n,)), dma((2,)),
             dma((2, ny)), dma((2, ny)), dma((2, ny)), dma((2, ny)),
             dma((cols_n,)), dma((2,)),
-            dma((2, n)), dma((2, n)),
-            dma((2, n)), dma((2, n)),
+            dma((2, CHUNKS, n)), dma((2, CHUNKS, n)),
+            dma((2, CHUNKS, n)), dma((2, CHUNKS, n)),
         ],
         compiler_params=pltpu.CompilerParams(
             collective_id=0, has_side_effects=True, vmem_limit_bytes=63 * 1024 * 1024),
         name="exchange",
-    )(send_idx, pivots, labels, tiles)
+    )(slot_tile, pivots, pivots, inverses, tiles)
 
     tiles_step = 2
     step = tiles_step * NB
@@ -695,21 +744,14 @@
         grid=(row_tiles // tiles_step,),
         out_shape=jax.ShapeDtypeStruct((2, rows, CBLK * NB), f32),
         in_specs=[
-            whole(2, NB), whole(2, 2, NB, NB), whole(4, NB, wide), whole(2, 4, NB, 2 * NB),
+            whole(2, NB), whole(4 * NB, wide), whole(4 * NB, wide), whole(2, 2 * NB, wide), whole(2, NB, wide),
             pl.BlockSpec((step, wide), lambda i: (i, 0)),
             pl.BlockSpec((2, tiles_step, NB, 2 * NB), lambda i: (0, i, 0, 0)),
         ],
         out_specs=pl.BlockSpec((2, step, CBLK * NB), lambda i: (0, i, 0)),
-        scratch_shapes=[
-            pltpu.VMEM((4 * NB, wide), f32),
-            pltpu.VMEM((4 * NB, wide), jnp.bfloat16),
-            pltpu.VMEM((4 * NB, wide), jnp.bfloat16),
-            pltpu.VMEM((3, 2 * NB, 2 * wide), jnp.bfloat16),
-            pltpu.VMEM((NB, wide), f32),
-        ],
         compiler_params=pltpu.CompilerParams(dimension_semantics=("arbitrary",), vmem_limit_bytes=63 * 1024 * 1024),
         name="finish",
-    )(pivots, inverses, fin, wfin, m_raw, ag.reshape(2, row_tiles, NB, 2 * NB))
+    )(pivots, hh, hl, done, tops, m_raw, ag.reshape(2, row_tiles, NB, 2 * NB))
 
 
 def grid_of(cols_n):

time: 159 us -> 152 us (0.956)
  Pallas kernels: 155 us -> 152 us
  other arithmetic: 2.86 us -> 0 us
    pallas_call x1, Pallas kernels: 15.4 us -> 11.1 us  [per_device(): pl.pallas_call(functools.partial(finish_kernel, rows_n, tiles_step), grid...]
where the time goes in v5:
time: 152 us
  Pallas kernels  152 us (100%)
    pallas_call x1, Pallas kernels, per_device(): pl.pallas_call(functools.partial(comm_kernel, dims), out_shape=(jax.Shape...  140 us
    pallas_call x1, Pallas kernels, per_device(): pl.pallas_call(functools.partial(finish_kernel, rows_n, tiles_step), grid...  11.1 us

profile of v5, /device:TPU:20, one launch (start us, length us, event | category | flops | bytes accessed | tf_op | source)
XLA Modules:
  0.0 151.5 jit_solution(687629579743536008)
XLA Ops:
  0.0 140.4 %exchange.1 = (f32[2048,512]{1,0:T(8,128)}, f32[2,4,4,128,256]{4,3,2,1,0:T(8,128)}, bf16[512,512]{1,0:T(8,128)(2,1)}, bf16[512,512]{1,0:T(8,128)(2,1)}, bf16[2,2...) custom-call(s32[1,32]{1,0:T(1,128)} %slot_ref.1, s32[2,128]{1,0:T(2,128)} %piv_ref.3, s32[2,128]{1,0:T(2,128)} %piv_ref.3, ...), custom_call_target="tpu_custom_call" | custom-call | tf_op jit(solution)/shard_map/exchange/pallas_call | solution.py:684
  140.4 11.1 %finish.1 = f32[2,2048,256]{2,1,0:T(8,128)} custom-call(s32[2,128]{1,0:T(2,128)} %piv_ref.3, bf16[512,512]{1,0:T(8,128)(2,1)} %get-tuple-element.11.h_hi, bf16[512,512]{1,0:T(8,128)(2,1)} %get-tuple-element.12.h_lo, bf16[2,256,512]{2,1,0:T(8,128)(2,1)} %get-tuple-element.13.done, f32[2,128,512]{2,1,0:T(8,128)} %get-tuple-element.14.tops, ...), custom_call_target="tpu_custom_call" | custom-call | tf_op jit(solution)/shard_map/finish/pallas_call | solution.py:742

commit v6 on v5

--- a/solution.py
+++ b/solution.py
@@ -16,10 +16,10 @@
 
 def comm_kernel(
     dims, slot_ref, piv_ref, piv_row, inv_ref, asm_hbm,
-    m_hbm, ag_hbm, hh_hbm, hl_hbm, done_hbm, tops_hbm,
-    asm, sendb, mid, recvb, labs, mat, pb, ag, st, pk, pr, ps, rb, fin, wfin, h, h_hi, h_lo, done, tops, plan, lab_ref, idx_ref, place,
+    m_hbm, ag_hbm, right_hbm, tops_hbm,
+    asm, sendb, mid, recvb, labs, mat, pb, ag, st, pk, pr, ps, rb, fin, wfin, h, right, tops, plan, lab_ref, idx_ref, place,
     out_sem, lab_s, lab_r, a_s, a_r, b_s, b_r, sx_s, sd_s, sr_s, st_r, sc_r, pk_s, pk_r, rs_s, rs_r, t_s, t_r,
-    y_s, y_r, k_s, k_r, wb_s, wb_r, g1_s, g1_r, g2_s, g2_r,
+    y_s, y_r, k_s, k_r, wb_s, wb_r, g1_s, g1_r, g2_s, g2_r, g_sem,
 ):
     rows_n, nx, nz, cap, row_tiles = dims
     cols_n = nx * nz
@@ -345,16 +345,6 @@
         for k in range(1, nx):
             g2x(ch, (me_x + k) % nx).start()
 
-    def gather_end(ch):
-        for k in range(1, nz):
-            sz = (me_z + k) % nz
-            part = ag.at[:, :, sz, part_rows(0, ch), :]
-            remote(part, part, g2_s.at[0, ch, sz], g2_r.at[0, ch, sz], me_r, me_x * nz + sz).wait_recv()
-        for k in range(1, nx):
-            sx = (me_x + k) % nx
-            part = ag.at[:, sx, :, part_rows(1, ch), :]
-            remote(part, part, g2_s.at[1, ch, sx], g2_r.at[1, ch, sx], me_r, sx * nz + me_z).wait_recv()
-
     def t_copy(s, d):
         rows = pl.ds(pl.multiple_of(d * sl, sl), sl)
         return remote(mat.at[rows, :], fin.at[2 + s, rows, :], t_s.at[d], t_r.at[s], d, me_c)
@@ -420,7 +410,16 @@
 
     def wb_copy(b, d):
         part = wfin.at[b, :, mine_rows, :]
-        return remote(part, part, wb_s.at[d], wb_r.at[b], me_r, d)
+        return remote(part, part, wb_s.at[b, d], wb_r.at[b], me_r, d)
+
+    def wb_root(b):
+        x0, z0 = root(b)
+        return ([wb_copy(b, (x0 + k) % nx * nz + z0) for k in range(1, nx)]
+                + [wb_copy(b, x0 * nz + (z0 + k) % nz) for k in range(1, nz)])
+
+    def wb_pass(b):
+        z0 = root(b)[1]
+        return [wb_copy(b, me_x * nz + (z0 + k) % nz) for k in range(1, nz)]
 
     for b in range(2):
         @pl.when(me_c == b)
@@ -428,10 +427,8 @@
             wfin[b, :, mine_rows, 0:NB] = fin[:, mine_rows, 0:NB]
             wfin[b, :, mine_rows, NB:2 * NB] = fin[:, mine_rows, CBLK * NB:(CBLK + 1) * NB]
 
-            def go(k, c):
-                wb_copy(b, (b + k) % cols_n).start()
-                return c
-            lax.fori_loop(1, cols_n, go, 0)
+            for copy in wb_root(b):
+                copy.start()
 
     def rows_of(w, r):
         rows = pl.ds(pl.multiple_of(r * sl, sl), sl)
@@ -464,31 +461,52 @@
 
     y_start(0)
 
+    def wb_wait(b):
+        part = wfin.at[b, :, mine_rows, :]
+        remote(part, part, wb_s.at[b, 0], wb_r.at[b], me_r, b).wait_recv()
+
+    for b in range(2):
+        @pl.when(is_relay_x(b))
+        def _():
+            wb_wait(b)
+            for copy in wb_pass(b):
+                copy.start()
+
     gather_second(0)
     for ch in range(1, CHUNKS):
         gather_first(ch)
         gather_second(ch)
 
     for b in range(2):
-        @pl.when(me_c != b)
-        def _():
-            part = wfin.at[b, :, mine_rows, :]
-            remote(part, part, wb_s.at[b], wb_r.at[b], me_r, b).wait_recv()
+        @pl.when((me_c != b) & jnp.logical_not(is_relay_x(b)))
+        def _():
+            wb_wait(b)
 
     y_start(1)
     y_pass(0)
     y_end(0)
     y_pass(1)
     y_end(1)
-    factors(piv_row, inv_ref, fin, wfin, me_c, h, h_hi, h_lo, done, tops)
+    factors(piv_row, inv_ref, fin, wfin, me_c, h, right, tops)
     small = [pltpu.make_async_copy(v, w, out_sem.at[1 + k]) for k, (v, w) in enumerate(
-        ((h_hi, hh_hbm), (h_lo, hl_hbm), (done, done_hbm), (tops, tops_hbm)))]
+        ((right, right_hbm), (tops, tops_hbm)))]
     for copy in small:
         copy.start()
-    for ch in range(CHUNKS):
-        gather_end(ch)
-    g_out = pltpu.make_async_copy(ag, ag_hbm, out_sem.at[5])
-    g_out.start()
+    outs = []
+    for k in range(nz):
+        sz = (me_z + k) % nz
+        part = ag.at[:, :, sz, part_rows(0, 0), :]
+        if k > 0:
+            remote(part, part, g2_s.at[0, 0, sz], g2_r.at[0, 0, sz], me_r, me_x * nz + sz).wait_recv()
+        outs.append(pltpu.make_async_copy(part, ag_hbm.at[:, :, sz, part_rows(0, 0), :], g_sem.at[0, k]))
+        outs[-1].start()
+        if k < nx:
+            sx = (me_x + k) % nx
+            part = ag.at[:, sx, :, part_rows(1, 0), :]
+            if k > 0:
+                remote(part, part, g2_s.at[1, 0, sx], g2_r.at[1, 0, sx], me_r, sx * nz + me_z).wait_recv()
+            outs.append(pltpu.make_async_copy(part, ag_hbm.at[:, sx, :, part_rows(1, 0), :], g_sem.at[1, k]))
+            outs[-1].start()
 
     def sent_col(k, c):
         d = (me_c + k) % cols_n
@@ -520,10 +538,13 @@
                 for copy in root_copies(b, ch):
                     copy.wait_send()
 
-            def go(k, c):
-                wb_copy(b, (b + k) % cols_n).wait_send()
-                return c
-            lax.fori_loop(1, cols_n, go, 0)
+            for copy in wb_root(b):
+                copy.wait_send()
+
+        @pl.when(is_relay_x(b))
+        def _():
+            for copy in wb_pass(b):
+                copy.wait_send()
 
         @pl.when(is_relay_x(b))
         def _():
@@ -553,7 +574,8 @@
     m_out.wait()
     for copy in small:
         copy.wait()
-    g_out.wait()
+    for copy in outs:
+        copy.wait()
 
 
 def cmat(v):
@@ -575,16 +597,18 @@
     return hi, (v - hi.astype(jnp.float32)).astype(jnp.bfloat16)
 
 
-def finished(own, panel, h_hi, h_lo, my_col):
-    wide = own.shape[1]
+def deep(panel):
     hi, lo = split(panel)
-    update = mm(hi, h_hi[...]) + (mm(hi, h_lo[...]) + mm(lo, h_hi[...]))
+    return jnp.concatenate([hi, hi, lo], 1)
+
+
+def keep(own, my_col):
     lane = lax.broadcasted_iota(jnp.int32, own.shape, 1)
-    first = ((lane % (wide // 2)) < NB) & (my_col < 2)
-    return jnp.where(first, 0.0, own) - update
-
-
-def factors(piv_ref, inv_ref, fin, wfin, my_col, h, h_hi, h_lo, done, tops):
+    first = ((lane % (own.shape[1] // 2)) < NB) & (my_col < 2)
+    return jnp.where(first, 0.0, own)
+
+
+def factors(piv_ref, inv_ref, fin, wfin, my_col, h, right, tops):
     wide = fin.shape[2]
     f32 = jnp.float32
     spots = (slice(0, NB), slice(wide // 2, wide // 2 + NB))
@@ -622,18 +646,19 @@
             h[0:2 * NB, lanes] = cg[:, k * NB:(k + 1) * NB]
             h[2 * NB:, lanes] = -ci[:, k * NB:(k + 1) * NB]
 
-    high, low = split(h[...])
-    h_hi[...] = high
-    h_lo[...] = low
+    high, low = split(-h[...])
+    right[0:wide] = high
+    right[wide:2 * wide] = low
+    right[2 * wide:3 * wide] = high
     rest = jnp.concatenate([fin[2], fin[3]], 0)
     panel = jnp.concatenate([jnp.concatenate([wfin[b, 2], wfin[b, 3]], 0) for b in range(2)], 1)
-    rest = finished(rest, panel, h_hi, h_lo, my_col)
+    rest = keep(rest, my_col) + mm(deep(panel), right[0:3 * wide])
     high, low = split(rest)
-    done[0] = high
-    done[1] = low
-
-
-def finish_kernel(rows_n, tiles_step, piv_ref, h_hi, h_lo, done, tops, m_ref, g_ref, o_ref):
+    right[3 * wide:3 * wide + 2 * NB] = high
+    right[3 * wide + 2 * NB:] = low
+
+
+def finish_kernel(rows_n, tiles_step, piv_ref, right, tops, m_ref, g_ref, o_ref):
     i = pl.program_id(0)
     my_col = lax.axis_index("pcol")
     my_row = lax.axis_index("prow")
@@ -648,9 +673,10 @@
     in0 = jnp.max(hit0, axis=1, keepdims=True)
     in1 = jnp.max(hit1, axis=1, keepdims=True)
     s = jnp.concatenate([hit0 * (1.0 - in1), hit1], 1).astype(bf16)
-    swap = mm(s, done[0]) + mm(s, done[1])
     panel = jnp.concatenate([g_ref[0].reshape(step, 2 * NB), g_ref[1].reshape(step, 2 * NB)], 1)
-    out = jnp.where(in0 + in1 > 0, swap, finished(m_ref[...], panel, h_hi, h_lo, my_col))
+    still = in0 + in1 == 0
+    left = jnp.concatenate([deep(jnp.where(still, panel, 0.0)), s, s], 1)
+    out = jnp.where(still, keep(m_ref[...], my_col), 0.0) + mm(left, right[...])
     for c in range(2):
         o_ref[c] = out[:, c * (wide // 2):(c + 1) * (wide // 2)]
 
@@ -681,18 +707,16 @@
     n = max(nx, nz)
     ny = rows_n // 2
     bf16 = jnp.bfloat16
-    m_raw, ag, hh, hl, done, tops = pl.pallas_call(
+    m_raw, ag, right, tops = pl.pallas_call(
         functools.partial(comm_kernel, dims),
         out_shape=(
             jax.ShapeDtypeStruct((rows, wide), f32),
             jax.ShapeDtypeStruct((2, nx, nz, NB, 2 * NB), f32),
-            jax.ShapeDtypeStruct((4 * NB, wide), bf16),
-            jax.ShapeDtypeStruct((4 * NB, wide), bf16),
-            jax.ShapeDtypeStruct((2, 2 * NB, wide), bf16),
+            jax.ShapeDtypeStruct((3 * wide + 4 * NB, wide), bf16),
             jax.ShapeDtypeStruct((2, NB, wide), f32),
         ),
         in_specs=[vmem, smem, vmem, vmem, hbm],
-        out_specs=(hbm,) * 6,
+        out_specs=(hbm,) * 4,
         scratch_shapes=[
             pltpu.VMEM((slots, 2, NB, NB), f32),
             pltpu.VMEM((2, cols_n, cap, NB, NB), f32),
@@ -710,9 +734,7 @@
             pltpu.VMEM((4, NB, wide), f32),
             pltpu.VMEM((2, 4, NB, 2 * NB), f32),
             pltpu.VMEM((4 * NB, wide), f32),
-            pltpu.VMEM((4 * NB, wide), bf16),
-            pltpu.VMEM((4 * NB, wide), bf16),
-            pltpu.VMEM((2, 2 * NB, wide), bf16),
+            pltpu.VMEM((3 * wide + 4 * NB, wide), bf16),
             pltpu.VMEM((2, NB, wide), f32),
             pltpu.VMEM((8, NB), jnp.int32),
             pltpu.VMEM((8, NB), jnp.int32),
@@ -727,16 +749,17 @@
             dma((ny,)), dma((ny,)),
             dma((rows_n,)), dma((2,)),
             dma((2, ny)), dma((2, ny)), dma((2, ny)), dma((2, ny)),
-            dma((cols_n,)), dma((2,)),
+            dma((2, cols_n)), dma((2,)),
             dma((2, CHUNKS, n)), dma((2, CHUNKS, n)),
             dma((2, CHUNKS, n)), dma((2, CHUNKS, n)),
+            dma((2, n)),
         ],
         compiler_params=pltpu.CompilerParams(
             collective_id=0, has_side_effects=True, vmem_limit_bytes=63 * 1024 * 1024),
         name="exchange",
     )(slot_tile, pivots, pivots, inverses, tiles)
 
-    tiles_step = 2
+    tiles_step = 4
     step = tiles_step * NB
     whole = lambda *shape: pl.BlockSpec(shape, lambda i: (0,) * len(shape))
     return pl.pallas_call(
@@ -744,14 +767,14 @@
         grid=(row_tiles // tiles_step,),
         out_shape=jax.ShapeDtypeStruct((2, rows, CBLK * NB), f32),
         in_specs=[
-            whole(2, NB), whole(4 * NB, wide), whole(4 * NB, wide), whole(2, 2 * NB, wide), whole(2, NB, wide),
+            whole(2, NB), whole(3 * wide + 4 * NB, wide), whole(2, NB, wide),
             pl.BlockSpec((step, wide), lambda i: (i, 0)),
             pl.BlockSpec((2, tiles_step, NB, 2 * NB), lambda i: (0, i, 0, 0)),
         ],
         out_specs=pl.BlockSpec((2, step, CBLK * NB), lambda i: (0, i, 0)),
         compiler_params=pltpu.CompilerParams(dimension_semantics=("arbitrary",), vmem_limit_bytes=63 * 1024 * 1024),
         name="finish",
-    )(pivots, hh, hl, done, tops, m_raw, ag.reshape(2, row_tiles, NB, 2 * NB))
+    )(pivots, right, tops, m_raw, ag.reshape(2, row_tiles, NB, 2 * NB))
 
 
 def grid_of(cols_n):

time: 152 us -> 145 us (0.954)
  Pallas kernels: 152 us -> 144 us
    pallas_call x1, Pallas kernels: 140 us -> 135 us  [per_device(): pl.pallas_call(functools.partial(comm_kernel, dims), out_shape=(jax.Shape...]
    pallas_call x1, Pallas kernels: 11.1 us -> 9.41 us  [per_device(): pl.pallas_call(functools.partial(finish_kernel, rows_n, tiles_step), grid...]
where the time goes in v6:
time: 145 us; the launch traced here: 144 us
  Pallas kernels  144 us (99%)
    pallas_call x1, Pallas kernels, per_device(): pl.pallas_call(functools.partial(comm_kernel, dims), out_shape=(jax.Shape...  135 us
    pallas_call x1, Pallas kernels, per_device(): pl.pallas_call(functools.partial(finish_kernel, rows_n, tiles_step), grid...  9.41 us

profile of v6, /device:TPU:20, one launch (start us, length us, event | category | flops | bytes accessed | tf_op | source)
XLA Modules:
  0.0 144.5 jit_solution(1018476156429062419)
XLA Ops:
  0.0 135.1 %exchange.1 = (f32[2048,512]{1,0:T(8,128)}, f32[2,4,4,128,256]{4,3,2,1,0:T(8,128)}, bf16[2048,512]{1,0:T(8,128)(2,1)}, f32[2,128,512]{2,1,0:T(8,128)}) custom-call(s32[1,32]{1,0:T(1,128)} %slot_ref.1, s32[2,128]{1,0:T(2,128)} %piv_ref.3, s32[2,128]{1,0:T(2,128)} %piv_ref.3, f32[2,2,128,128]{3,2,1,0:T(8,128)} %inv_ref.1, f32[32,2,128,128]{3,2,1,0:T(8,128)} %bitcast.2), custom_call_target="tpu_custom_call" | custom-call | tf_op jit(solution)/shard_map/exchange/pallas_call | solution.py:710
  135.1 9.4 %finish.1 = f32[2,2048,256]{2,1,0:T(8,128)} custom-call(s32[2,128]{1,0:T(2,128)} %piv_ref.3, bf16[2048,512]{1,0:T(8,128)(2,1)} %get-tuple-element.9.right, f32[2,128,512]{2,1,0:T(8,128)} %get-tuple-element.10.tops, f32[2048,512]{1,0:T(8,128)} %get-tuple-element.11.m_ref, f32[2,16,128,256]{3,2,1,0:T(8,128)} %bitcast.3), custom_call_target="tpu_custom_call" | custom-call | tf_op jit(solution)/shard_map/finish/pallas_call | solution.py:765

commit v7 on v6

--- a/solution.py
+++ b/solution.py
@@ -19,7 +19,7 @@
     m_hbm, ag_hbm, right_hbm, tops_hbm,
     asm, sendb, mid, recvb, labs, mat, pb, ag, st, pk, pr, ps, rb, fin, wfin, h, right, tops, plan, lab_ref, idx_ref, place,
     out_sem, lab_s, lab_r, a_s, a_r, b_s, b_r, sx_s, sd_s, sr_s, st_r, sc_r, pk_s, pk_r, rs_s, rs_r, t_s, t_r,
-    y_s, y_r, k_s, k_r, wb_s, wb_r, g1_s, g1_r, g2_s, g2_r, g_sem,
+    y_s, y_r, k_s, k_r, wb_s, wb_r, g1_s, g1_r, g2_s, g2_r, g3_s, g_sem,
 ):
     rows_n, nx, nz, cap, row_tiles = dims
     cols_n = nx * nz
@@ -193,25 +193,6 @@
 
     lax.fori_loop(1, cols_n, a_wait, 0)
 
-    def put(i, c):
-        rows = pl.ds(pl.multiple_of(i * NB, NB), NB)
-        for m in range(CBLK):
-            at = place[i * CBLK + m]
-            s = at // cap
-            r = at - s * cap
-            re = recvb[0, s, r]
-            im = recvb[1, s, r]
-            mat[rows, m * NB:(m + 1) * NB] = re
-            mat[rows, (CBLK + m) * NB:(CBLK + m + 1) * NB] = im
-            if m == 0:
-                pb[i // nz, i % nz, :, 0:NB] = re
-                pb[i // nz, i % nz, :, NB:2 * NB] = im
-        return c
-
-    lax.fori_loop(0, row_tiles, put, 0)
-    m_out = pltpu.make_async_copy(mat, m_hbm, out_sem.at[0])
-    m_out.start()
-
     piece = NB // (2 * CHUNKS)
 
     def part_rows(kind, ch):
@@ -234,7 +215,7 @@
     def root_copies(b, ch):
         x0, z0 = root(b)
         copies = []
-        for k in range(1, max(nx, nz)):
+        for k in sorted(range(1, max(nx, nz)), key=lambda k: abs(k - nx // 2)):
             if k < nx:
                 copies.append(out_x(b, ch, (x0 + k) % nx))
             if k < nz:
@@ -268,6 +249,15 @@
     for b in range(2):
         @pl.when(me_c == b)
         def _():
+            def panel(i, c):
+                at = place[i * CBLK]
+                s = at // cap
+                r = at - s * cap
+                pb[i // nz, i % nz, :, 0:NB] = recvb[0, s, r]
+                pb[i // nz, i % nz, :, NB:2 * NB] = recvb[1, s, r]
+                return c
+
+            lax.fori_loop(0, row_tiles, panel, 0)
             for ch in range(CHUNKS):
                 for copy in root_copies(b, ch):
                     copy.start()
@@ -301,13 +291,35 @@
         part = ag.at[:, me_x, me_z, part_rows(1, ch), :]
         return remote(part, part, g1_s.at[1, ch, dz], g1_r.at[1, ch, me_z], me_r, me_x * nz + dz)
 
-    def g2z(ch, dz):
-        part = ag.at[:, :, me_z, part_rows(0, ch), :]
-        return remote(part, part, g2_s.at[0, ch, dz], g2_r.at[0, ch, me_z], me_r, me_x * nz + dz)
-
-    def g2x(ch, dx):
-        part = ag.at[:, me_x, :, part_rows(1, ch), :]
-        return remote(part, part, g2_s.at[1, ch, dx], g2_r.at[1, ch, me_x], me_r, dx * nz + me_z)
+    def g2z(sx, b, way):
+        part = ag.at[b, sx, me_z, part_rows(0, 0), :]
+        return remote(part, part, g2_s.at[0, sx, b, way], g2_r.at[0, sx, b, me_z],
+                      me_r, me_x * nz + (me_z + (1, nz - 1)[way]) % nz)
+
+    def g2x(sz, b, way):
+        part = ag.at[b, me_x, sz, part_rows(1, 0), :]
+        return remote(part, part, g2_s.at[1, sz, b, way], g2_r.at[1, sz, b, me_x],
+                      me_r, (me_x + (1, nx - 1)[way]) % nx * nz + me_z)
+
+    def g2z_in(sx, b, sz):
+        part = ag.at[b, sx, sz, part_rows(0, 0), :]
+        return remote(part, part, g3_s.at[0, sx, b], g2_r.at[0, sx, b, sz], me_r, me_x * nz + sz)
+
+    def g2x_in(sz, b, sx):
+        part = ag.at[b, sx, sz, part_rows(1, 0), :]
+        return remote(part, part, g3_s.at[1, sz, b], g2_r.at[1, sz, b, sx], me_r, sx * nz + me_z)
+
+    def g3z(sx, b):
+        sz = (me_z + (nz - 1, 1)[b]) % nz
+        part = ag.at[b, sx, sz, part_rows(0, 0), :]
+        return remote(part, part, g3_s.at[0, sx, b], g2_r.at[0, sx, b, sz],
+                      me_r, me_x * nz + (me_z + (1, nz - 1)[b]) % nz)
+
+    def g3x(sz, b):
+        sx = (me_x + (nx - 1, 1)[b]) % nx
+        part = ag.at[b, sx, sz, part_rows(1, 0), :]
+        return remote(part, part, g3_s.at[1, sz, b], g2_r.at[1, sz, b, sx],
+                      me_r, (me_x + (1, nx - 1)[b]) % nx * nz + me_z)
 
     def gather_first(ch):
         for b in range(2):
@@ -321,6 +333,9 @@
         for k in range(1, nx):
             g1x(ch, (me_x + k) % nx).start()
         for b in range(2):
+            for way in range(2):
+                g2z(me_x, b, way).start()
+        for b in range(2):
             x0 = root(b)[0]
 
             @pl.when(me_x != x0)
@@ -330,20 +345,50 @@
 
         for k in range(1, nz):
             g1z(ch, (me_z + k) % nz).start()
+        for b in range(2):
+            for way in range(2):
+                g2x(me_z, b, way).start()
 
     def gather_second(ch):
-        for k in range(1, nx):
-            sx = (me_x + k) % nx
+        for j in range(1, max(nx, nz)):
+            sx = (me_x + j) % nx
             part = ag.at[:, sx, me_z, part_rows(0, ch), :]
             remote(part, part, g1_s.at[0, ch, sx], g1_r.at[0, ch, sx], me_r, sx * nz + me_z).wait_recv()
-        for k in range(1, nz):
-            g2z(ch, (me_z + k) % nz).start()
-        for k in range(1, nz):
-            sz = (me_z + k) % nz
+            for b in range(2):
+                for way in range(2):
+                    g2z(sx, b, way).start()
+            sz = (me_z + j) % nz
             part = ag.at[:, me_x, sz, part_rows(1, ch), :]
             remote(part, part, g1_s.at[1, ch, sz], g1_r.at[1, ch, sz], me_r, me_x * nz + sz).wait_recv()
-        for k in range(1, nx):
-            g2x(ch, (me_x + k) % nx).start()
+            for b in range(2):
+                for way in range(2):
+                    g2x(sz, b, way).start()
+
+    def gather_third(ch):
+        for j in range(nx):
+            for b in range(2):
+                sx = (me_x + j) % nx
+                g2z_in(sx, b, (me_z + (nz - 1, 1)[b]) % nz).wait_recv()
+                g3z(sx, b).start()
+                sz = (me_z + j) % nz
+                g2x_in(sz, b, (me_x + (nx - 1, 1)[b]) % nx).wait_recv()
+                g3x(sz, b).start()
+
+    def put(i, c):
+        rows = pl.ds(pl.multiple_of(i * NB, NB), NB)
+        for m in range(CBLK):
+            at = place[i * CBLK + m]
+            s = at // cap
+            r = at - s * cap
+            re = recvb[0, s, r]
+            im = recvb[1, s, r]
+            mat[rows, m * NB:(m + 1) * NB] = re
+            mat[rows, (CBLK + m) * NB:(CBLK + m + 1) * NB] = im
+        return c
+
+    lax.fori_loop(0, row_tiles, put, 0)
+    m_out = pltpu.make_async_copy(mat, m_hbm, out_sem.at[0])
+    m_out.start()
 
     def t_copy(s, d):
         rows = pl.ds(pl.multiple_of(d * sl, sl), sl)
@@ -484,6 +529,7 @@
 
     y_start(1)
     y_pass(0)
+    gather_third(0)
     y_end(0)
     y_pass(1)
     y_end(1)
@@ -493,20 +539,29 @@
     for copy in small:
         copy.start()
     outs = []
-    for k in range(nz):
+
+    def out_lo(k, sz):
+        outs.append(pltpu.make_async_copy(ag.at[:, :, sz, part_rows(0, 0), :], ag_hbm.at[:, :, sz, part_rows(0, 0), :],
+                                          g_sem.at[0, k]))
+        outs[-1].start()
+
+    def out_hi(k, sx):
+        outs.append(pltpu.make_async_copy(ag.at[:, sx, :, part_rows(1, 0), :], ag_hbm.at[:, sx, :, part_rows(1, 0), :],
+                                          g_sem.at[1, k]))
+        outs[-1].start()
+
+    out_lo(0, me_z)
+    out_hi(0, me_x)
+    for k in (1, nz - 1, nz // 2):
         sz = (me_z + k) % nz
-        part = ag.at[:, :, sz, part_rows(0, 0), :]
-        if k > 0:
-            remote(part, part, g2_s.at[0, 0, sz], g2_r.at[0, 0, sz], me_r, me_x * nz + sz).wait_recv()
-        outs.append(pltpu.make_async_copy(part, ag_hbm.at[:, :, sz, part_rows(0, 0), :], g_sem.at[0, k]))
-        outs[-1].start()
-        if k < nx:
-            sx = (me_x + k) % nx
-            part = ag.at[:, sx, :, part_rows(1, 0), :]
-            if k > 0:
-                remote(part, part, g2_s.at[1, 0, sx], g2_r.at[1, 0, sx], me_r, sx * nz + me_z).wait_recv()
-            outs.append(pltpu.make_async_copy(part, ag_hbm.at[:, sx, :, part_rows(1, 0), :], g_sem.at[1, k]))
-            outs[-1].start()
+        sx = (me_x + k) % nx
+        for b in range(2):
+            if k == nz // 2 or b == (0 if k == 1 else 1):
+                for j in range(nx):
+                    g2z_in(j, b, sz).wait_recv()
+                    g2x_in(j, b, sx).wait_recv()
+        out_lo(k, sz)
+        out_hi(k, sx)
 
     def sent_col(k, c):
         d = (me_c + k) % cols_n
@@ -567,10 +622,15 @@
     for ch in range(CHUNKS):
         for k in range(1, nx):
             g1x(ch, (me_x + k) % nx).wait_send()
-            g2x(ch, (me_x + k) % nx).wait_send()
         for k in range(1, nz):
             g1z(ch, (me_z + k) % nz).wait_send()
-            g2z(ch, (me_z + k) % nz).wait_send()
+    for j in range(nx):
+        for b in range(2):
+            for way in range(2):
+                g2z(j, b, way).wait_send()
+                g2x(j, b, way).wait_send()
+            g3z(j, b).wait_send()
+            g3x(j, b).wait_send()
     m_out.wait()
     for copy in small:
         copy.wait()
@@ -751,7 +811,7 @@
             dma((2, ny)), dma((2, ny)), dma((2, ny)), dma((2, ny)),
             dma((2, cols_n)), dma((2,)),
             dma((2, CHUNKS, n)), dma((2, CHUNKS, n)),
-            dma((2, CHUNKS, n)), dma((2, CHUNKS, n)),
+            dma((2, n, 2, 2)), dma((2, n, 2, n)), dma((2, n, 2)),
             dma((2, n)),
         ],
         compiler_params=pltpu.CompilerParams(

time: 145 us -> 143 us (0.986); the launches traced: 144 us -> 141 us
  Pallas kernels: 144 us -> 141 us
    pallas_call x1, Pallas kernels: 135 us -> 131 us  [per_device(): pl.pallas_call(functools.partial(comm_kernel, dims), out_shape=(jax.Shape...]
where the time goes in v7:
time: 143 us; the launch traced here: 141 us
  Pallas kernels  141 us (99%)
    pallas_call x1, Pallas kernels, per_device(): pl.pallas_call(functools.partial(comm_kernel, dims), out_shape=(jax.Shape...  131 us
    pallas_call x1, Pallas kernels, per_device(): pl.pallas_call(functools.partial(finish_kernel, rows_n, tiles_step), grid...  9.42 us

profile of v7, /device:TPU:20, one launch (start us, length us, event | category | flops | bytes accessed | tf_op | source)
XLA Modules:
  0.0 140.7 jit_solution(16634552081840886207)
XLA Ops:
  0.0 131.2 %exchange.1 = (f32[2048,512]{1,0:T(8,128)}, f32[2,4,4,128,256]{4,3,2,1,0:T(8,128)}, bf16[2048,512]{1,0:T(8,128)(2,1)}, f32[2,128,512]{2,1,0:T(8,128)}) custom-call(s32[1,32]{1,0:T(1,128)} %slot_ref.1, s32[2,128]{1,0:T(2,128)} %piv_ref.3, s32[2,128]{1,0:T(2,128)} %piv_ref.3, f32[2,2,128,128]{3,2,1,0:T(8,128)} %inv_ref.1, f32[32,2,128,128]{3,2,1,0:T(8,128)} %bitcast.2), custom_call_target="tpu_custom_call" | custom-call | tf_op jit(solution)/shard_map/exchange/pallas_call | solution.py:770
  131.2 9.4 %finish.1 = f32[2,2048,256]{2,1,0:T(8,128)} custom-call(s32[2,128]{1,0:T(2,128)} %piv_ref.3, bf16[2048,512]{1,0:T(8,128)(2,1)} %get-tuple-element.9.right, f32[2,128,512]{2,1,0:T(8,128)} %get-tuple-element.10.tops, f32[2048,512]{1,0:T(8,128)} %get-tuple-element.11.m_ref, f32[2,16,128,256]{3,2,1,0:T(8,128)} %bitcast.3), custom_call_target="tpu_custom_call" | custom-call | tf_op jit(solution)/shard_map/finish/pallas_call | solution.py:825

commit v8 on v7

--- a/solution.py
+++ b/solution.py
@@ -529,9 +529,9 @@
 
     y_start(1)
     y_pass(0)
-    gather_third(0)
     y_end(0)
     y_pass(1)
+    gather_third(0)
     y_end(1)
     factors(piv_row, inv_ref, fin, wfin, me_c, h, right, tops)
     small = [pltpu.make_async_copy(v, w, out_sem.at[1 + k]) for k, (v, w) in enumerate(
@@ -819,7 +819,7 @@
         name="exchange",
     )(slot_tile, pivots, pivots, inverses, tiles)
 
-    tiles_step = 4
+    tiles_step = 8
     step = tiles_step * NB
     whole = lambda *shape: pl.BlockSpec(shape, lambda i: (0,) * len(shape))
     return pl.pallas_call(

time: 143 us -> 142 us (level)
  no operation moved by 1% of the time
where the time goes in v8:
time: 142 us; the launch traced here: 140 us
  Pallas kernels  140 us (99%)
    pallas_call x1, Pallas kernels, per_device(): pl.pallas_call(functools.partial(comm_kernel, dims), out_shape=(jax.Shape...  131 us
    pallas_call x1, Pallas kernels, per_device(): pl.pallas_call(functools.partial(finish_kernel, rows_n, tiles_step), grid...  9.18 us

profile of v8, /device:TPU:20, one launch (start us, length us, event | category | flops | bytes accessed | tf_op | source)
XLA Modules:
  0.0 140.0 jit_solution(7266189950027883806)
XLA Ops:
  0.0 130.8 %exchange.1 = (f32[2048,512]{1,0:T(8,128)}, f32[2,4,4,128,256]{4,3,2,1,0:T(8,128)}, bf16[2048,512]{1,0:T(8,128)(2,1)}, f32[2,128,512]{2,1,0:T(8,128)}) custom-call(s32[1,32]{1,0:T(1,128)} %slot_ref.1, s32[2,128]{1,0:T(2,128)} %piv_ref.3, s32[2,128]{1,0:T(2,128)} %piv_ref.3, f32[2,2,128,128]{3,2,1,0:T(8,128)} %inv_ref.1, f32[32,2,128,128]{3,2,1,0:T(8,128)} %bitcast.2), custom_call_target="tpu_custom_call" | custom-call | tf_op jit(solution)/shard_map/exchange/pallas_call | solution.py:770
  130.8 9.2 %finish.1 = f32[2,2048,256]{2,1,0:T(8,128)} custom-call(s32[2,128]{1,0:T(2,128)} %piv_ref.3, bf16[2048,512]{1,0:T(8,128)(2,1)} %get-tuple-element.9.right, f32[2,128,512]{2,1,0:T(8,128)} %get-tuple-element.10.tops, f32[2048,512]{1,0:T(8,128)} %get-tuple-element.11.m_ref, f32[2,16,128,256]{3,2,1,0:T(8,128)} %bitcast.3), custom_call_target="tpu_custom_call" | custom-call | tf_op jit(solution)/shard_map/finish/pallas_call | solution.py:825
